TPU v7x, 512 devices: a whole 4x8x8 slice. The times are simulated.
512 devices in a mesh: row: 16 (over z_hi, y), rhs: 32 (over x, z_lo, core).
Axes of the slice: x: 4, y: 8, z: 8 (z_hi: 2, z_lo: 4; z = z_hi * 4 + z_lo), core: 2. Of those that a mesh axis runs over, the one named last changes fastest.
Arguments:
- factor: bfloat16 [2, 8192, 512], P(None, 'row', 'rhs'), may hold values from -0.25 to 0.25
- pivots: float32 [2, 512], replicated, may hold values from 2 to 3
- right_sides: float32 [8192, 4096], P('row', 'rhs'), may hold values from -6 to 6
Outputs:
- solved: float32 [8192, 4096], P('row', 'rhs')
All inputs are finite; a program needn't handle non-finite values.
Results may differ from a plain program's by a relative error of at most 0.0003.
Values may be sent and summed in bfloat16 or wider, within the bound.
No kernel may reach another device: no remote copies, remote signals or barrier semaphores. Data moves between devices by JAX's collectives and lax.ppermute only.
A program may use at most 64 MiB of HBM per device.

v0:
```python
import jax
import jax.numpy as jnp
from jax import lax
from jax.sharding import Mesh
from jax.sharding import PartitionSpec as P

ROW = ("row_0", "row_1")


def broadcast_by_axis(shard, axes, root):
    shard = jnp.where(lax.axis_index(axes) == root, shard, jnp.zeros_like(shard))
    for axis in axes:
        shard = lax.psum(shard, axis)
    return shard


def copy_for_each(shard, axis):
    count = lax.axis_size(axis)
    return lax.all_to_all(
        jnp.broadcast_to(shard[None], (count, *shard.shape)), axis, 0, 0, tiled=True
    )


def in_order(parts, dim):
    dims = list(parts.shape[1:])
    dims[dim] *= parts.shape[0]
    return jnp.moveaxis(parts, 0, dim).reshape(dims)


def collect(shard, axis, dim):
    parts = copy_for_each(shard, axis)
    return in_order(parts, dim)


def solve_block(panel_rows, pivot_row, resid_rows):
    block = panel_rows.astype(jnp.float32)
    diag_k = jnp.tril(block, -1) + jnp.diag(pivot_row)
    return lax.linalg.triangular_solve(diag_k, resid_rows, left_side=True, lower=True)


def spread(candidate, owner):
    return broadcast_by_axis(candidate, ROW, owner)


def advance(resid, panel, solved_rows, global_row, index, offset):
    width = solved_rows.shape[0]
    update = jnp.dot(
        panel.astype(jnp.float32),
        solved_rows,
        precision=lax.Precision.HIGHEST,
        preferred_element_type=jnp.float32,
    )
    placed = resid.at[offset : offset + width].set(solved_rows)
    inside = (global_row >= index * width) & (global_row < (index + 1) * width)
    lower = global_row >= (index + 1) * width
    return jnp.where(lower, resid - update, jnp.where(inside, placed, resid))


def body(factor, pivots, right_sides):
    rows = right_sides.shape[0]
    width = pivots.shape[1]
    count = pivots.shape[0]
    global_row = lax.axis_index(ROW) * rows + lax.broadcasted_iota(jnp.int32, (rows, 1), 0)
    every_panel = collect(factor, "rhs", 2)
    resid = right_sides
    for index in range(count):
        panel = every_panel[index]
        owner = index * width // rows
        offset = index * width % rows
        candidate = solve_block(panel, pivots[index], resid)
        solved_rows = spread(candidate, owner)
        resid = advance(resid, panel, solved_rows, global_row, index, offset)
    return resid


def solution(mesh):
    split = Mesh(mesh.devices.reshape(2, 8, mesh.shape["rhs"]), ("row_0", "row_1", "rhs"))
    return jax.shard_map(
        body,
        mesh=split,
        in_specs=(P(None, ROW, "rhs"), P(), P(ROW, "rhs")),
        out_specs=P(ROW, "rhs"),
        check_vma=False,
    )
```

profile of v0, /device:TPU:2, one launch (start us, length us, event | category | flops | bytes accessed | tf_op | source)
XLA Modules:
  0.0 370.5 jit_solution(5300908107925342727)
XLA Ops:
  6.5 1.9 broadcast_in_dim.63
  8.4 10.4 %all-to-all-start = ((bf16[32,2,512,16]{2,3,1,0:T(8,128)(2,1)}), bf16[32,2,512,16]{2,3,1,0:T(8,128)(2,1)S(1)}, u32[]{:S(2)}, u32[]{:S(2)}) async-start(bf16[32,2,512,16]{2,3,1,0:T(8,128)(2,1)} %broadcast_in_dim.63), calls=%async_computation | async-start | bytes 2097152 | tf_op jit(solution)/shard_map/all_to_all | solution.py:19
  18.9 0.7 copy-done.2
  19.6 24.6 %all-to-all-done = bf16[32,2,512,16]{2,3,1,0:T(8,128)(2,1)S(1)} async-done(((bf16[32,2,512,16]{2,3,1,0:T(8,128)(2,1)}), bf16[32,2,512,16]{2,3,1,0:T(8,128)(2,1)S(1)}, u32[]{:S(2)}, u32[]{:S(2)}) %all-to-all-start) | async-done | bytes 1048608 | tf_op jit(solution)/shard_map/all_to_all | solution.py:19
  44.7 0.7 broadcast.129.clone
  45.4 10.9 %while.8 = (s32[]{:T(128)}, f32[512,512]{0,1:T(8,128)S(1)}, s32[4,2]{0,1:T(2,128)S(1)}, f32[4,128,128]{2,1,0:T(8,128)}, s32[]{:T(128)}) while((s32[]{:T(128)}, f32[512,512]{0,1:T(8,128)S(1)}, s32[4,2]{0,1:T(2,128)S(1)}, f32[4,128,128]{2,1,0:T(8,128)}, s32[]{:T(128)}) %tuple.58), condition=%wide.while_cond.2, body=%wide.while_body.2.sunk | while | flops 2 | bytes 393829 | solution.py:38
  45.5 0.6 fusion.67
  46.1 1.3 dynamic-slice.22
  47.5 0.6 bitcast_dynamic-update-slice_fusion.4
  48.2 0.6 fusion.67
  48.8 1.3 dynamic-slice.22
  50.2 0.6 bitcast_dynamic-update-slice_fusion.4
  51.5 1.3 dynamic-slice.22
  53.0 0.6 bitcast_dynamic-update-slice_fusion.4
  54.3 1.3 dynamic-slice.22
  55.7 0.6 bitcast_dynamic-update-slice_fusion.4
  56.3 40.8 %custom-call.4 = f32[4,128,128]{1,2,0:T(8,128)} custom-call(f32[4,128,128]{2,1,0:T(8,128)} %get-tuple-element.60), custom_call_target="InvertDiagBlocksLowerTriangular" | custom-call | tf_op jit(solution)/shard_map/triangular_solve/custom-call.1 | solution.py:38
  97.1 1.2 fusion.36
  100.4 0.7 maximum_select_fusion
  101.2 53.0 %all-reduce.5.cloned.1.call-done = f32[512,128]{1,0:T(8,128)} async-done(((f32[512,128]{1,0:T(8,128)}), f32[512,128]{1,0:T(8,128)}) %all-reduce.5.cloned.1.call-update) | async-done | bytes 262160 | tf_op jit(solution)/shard_map/psum | solution.py:13
  154.2 8.1 %while.9 = (s32[]{:T(128)}, f32[512,512]{0,1:T(8,128)S(1)}, s32[4,2]{0,1:T(2,128)S(1)}, f32[4,128,128]{2,1,0:T(8,128)S(1)}, s32[]{:T(128)}) while((s32[]{:T(128)}, f32[512,512]{0,1:T(8,128)S(1)}, s32[4,2]{0,1:T(2,128)S(1)}, f32[4,128,128]{2,1,0:T(8,128)S(1)}, s32[]{:T(128)}) %tuple.72), condition=%wide.while_cond.2.clone, body=%wide.while_body.2.clone.sunk | while | flops 2 | bytes 393321 | solution.py:38
  154.8 1.3 dynamic-slice.24
  156.9 1.3 dynamic-slice.24
  158.9 1.3 dynamic-slice.24
  160.9 1.3 dynamic-slice.24
  162.3 39.3 %custom-call.5 = f32[4,128,128]{1,2,0:T(8,128)S(1)} custom-call(f32[4,128,128]{2,1,0:T(8,128)S(1)} %get-tuple-element.61), custom_call_target="InvertDiagBlocksLowerTriangular" | custom-call | tf_op jit(solution)/shard_map/triangular_solve/custom-call.1 | solution.py:38
  201.6 29.4 %all-reduce.7.cloned.1.call-done = f32[512,128]{1,0:T(8,128)} async-done(((f32[512,128]{1,0:T(8,128)}), f32[512,128]{1,0:T(8,128)}) %all-reduce.7.cloned.1.call-update) | async-done | bytes 262160 | tf_op jit(solution)/shard_map/psum | solution.py:13
  231.0 1.8 fusion.2
  235.1 0.7 maximum_select_fusion.1
  235.9 49.1 %all-reduce.9.cloned.1.call-done = f32[512,128]{1,0:T(8,128)} async-done(((f32[512,128]{1,0:T(8,128)}), f32[512,128]{1,0:T(8,128)}) %all-reduce.9.cloned.1.call-update) | async-done | bytes 262160 | tf_op jit(solution)/shard_map/psum | solution.py:13
  285.1 76.4 %all-reduce.11.cloned.1.call-done = f32[512,128]{1,0:T(8,128)} async-done(((f32[512,128]{1,0:T(8,128)}), f32[512,128]{1,0:T(8,128)}) %all-reduce.11.cloned.1.call-update) | async-done | bytes 262160 | tf_op jit(solution)/shard_map/psum | solution.py:13
  361.5 2.5 fusion.3
  (62 shorter events, 9.7 us)
Async XLA Ops:
  8.4 35.7 %all-to-all-start = ((bf16[32,2,512,16]{2,3,1,0:T(8,128)(2,1)}), bf16[32,2,512,16]{2,3,1,0:T(8,128)(2,1)S(1)}, u32[]{:S(2)}, u32[]{:S(2)}) async-start(bf16[32,2,512,16]{2,3,1,0:T(8,128)(2,1)} %broadcast_in_dim.63), calls=%async_computation | async-start | bytes 2097152 | tf_op jit(solution)/shard_map/all_to_all | solution.py:19
  18.8 135.3 %all-reduce.5.cloned.1.call-start = ((), (), s32[]{:S(2)}) async-start(), calls=%async_computation.1 | async-start | bytes 524288 | tf_op jit(solution)/shard_map/psum | solution.py:13
  18.9 0.7 copy-start.2
  45.4 51.7 %copy-start = (f32[512,128]{1,0:T(8,128)S(1)}, f32[512,128]{1,0:T(8,128)}, u32[]{:S(2)}) copy-start(f32[512,128]{1,0:T(8,128)} %param.15) | copy-start | bytes 786436
  97.1 1.5 copy-start.1
  101.1 129.9 %all-reduce.7.cloned.1.call-start = ((), (), s32[]{:S(2)}) async-start(), calls=%async_computation.2 | async-start | bytes 524288 | tf_op jit(solution)/shard_map/psum | solution.py:13
  154.2 130.9 %all-reduce.9.cloned.1.call-start = ((), (), s32[]{:S(2)}) async-start(), calls=%async_computation.3 | async-start | bytes 524288 | tf_op jit(solution)/shard_map/psum | solution.py:13
  235.9 125.6 %all-reduce.11.cloned.1.call-start = ((), (), s32[]{:S(2)}) async-start(), calls=%async_computation.4 | async-start | bytes 524288 | tf_op jit(solution)/shard_map/psum | solution.py:13
Sparse Core Ops, SparseCore 0:
  101.2 52.8 all-reduce.4
  156.4 74.5 all-reduce.6
  236.0 48.9 all-reduce.8
  287.2 74.2 all-reduce.10
where the time goes:
time: 371 us; the launch traced here: 370 us
  waiting for transfers between devices  232 us (63%)
  other arithmetic  81.9 us (22%)
  local copies, waits for them, and re-layouts  22.2 us (6%)
  between operations  13.4 us (4%)
  starting transfers between devices  10.6 us (3%)
  matrix products  9.74 us (3%)
    psum x4, waiting for transfers between devices, broadcast_by_axis(): shard = lax.psum(shard, axis)  208 us
    another operation x4, other arithmetic, solve_block(): lax.linalg.triangular_solve(diag_k, resid_rows, left_side=True, lower=True)  80.4 us
    all_to_all x1, waiting for transfers between devices, copy_for_each(): lax.all_to_all(jnp.broadcast_to(shard[None], (count, *shard.shape)), axis...  24.6 us
    another operation x43, local copies, waits for them, and re-layouts, solve_block(): lax.linalg.triangular_solve(diag_k, resid_rows, left_side=True, lower=True)  19.5 us
    all_to_all x1, starting transfers between devices, copy_for_each(): lax.all_to_all(jnp.broadcast_to(shard[None], (count, *shard.shape)), axis...  10.4 us
  transfers between devices with their start and end apart: 5, of which 5 were waited for; matrix products, arithmetic and copies ran while one was open for 13% of the time, Pallas kernels for 0%

commit v1 on v0

v1 whole, which is shorter than its diff:
```python
import functools

import jax
import jax.numpy as jnp
from jax import lax
from jax.experimental import pallas as pl
from jax.experimental.pallas import tpu as pltpu
from jax.sharding import Mesh
from jax.sharding import PartitionSpec as P

ROW = ("zh", "y")
RHS = ("x", "zl", "c")
F32, BF16 = jnp.float32, jnp.bfloat16
BASE, BLK = 32, 128


def split2(v):
    hi = v.astype(BF16)
    lo = (v - hi.astype(F32)).astype(BF16)
    return hi, lo


def mm(a, b):
    return jnp.dot(a, b, preferred_element_type=F32)


def dot_exact_left(a, v):
    n = v.shape[1]
    both = mm(a, jnp.concatenate(split2(v), axis=1))
    return both[:, :n] + both[:, n:]


def dot_exact_right(v, b):
    m = v.shape[0]
    both = mm(jnp.concatenate(split2(v), axis=0), b)
    return both[:m] + both[m:]


def dot3(a, b):
    n = b.shape[1]
    ah, al = split2(a)
    bh, bl = split2(b)
    both = mm(ah, jnp.concatenate([bh, bl], axis=1))
    return both[:, :n] + (both[:, n:] + mm(al, bh))


def iota(shape, dim):
    return lax.broadcasted_iota(jnp.int32, shape, dim)


def invert_blocks(low, recip):
    count = len(low)
    row, lane = iota((BLK, BLK), 0), iota((BLK, BLK), 1)
    seg = lane // BASE
    packed = []
    for blk in low:
        strict = jnp.where(row > lane, blk, 0.0)
        part = jnp.zeros((BASE, BLK), F32)
        for s in range(BLK // BASE):
            part = jnp.where(seg[:BASE] == s, strict[s * BASE : (s + 1) * BASE], part)
        packed.append(part)
    packed = jnp.concatenate(packed, axis=0).astype(BF16)
    pick = row - seg * BASE
    r = [jnp.where(pick[:BASE] + seg[:BASE] * BASE == lane[:BASE] % BASE, 1.0, 0.0).astype(F32) for _ in range(count)]
    for i in range(BASE - 1):
        spread = mm(packed, jnp.where(pick == i, 1.0, 0.0).astype(BF16))
        top = (i + 1) // 8 * 8
        for k in range(count):
            x = r[k][i : i + 1] * recip[k, i : i + 1]
            tail = r[k][top:] - spread[k * BASE + top : (k + 1) * BASE] * x
            r[k] = jnp.concatenate([r[k][:top], tail], axis=0) if top else tail
    out = []
    for k in range(count):
        x = r[k] * recip[k]
        x = jnp.where(row // BASE == seg, jnp.concatenate([x] * (BLK // BASE), axis=0), 0.0)
        size = BASE
        while size < BLK:
            off = (row // size > lane // size) & (row // (2 * size) == lane // (2 * size))
            off = jnp.where(off, low[k], 0.0).astype(BF16)
            x = x - dot3(dot_exact_right(x, off), x)
            size *= 2
        out.append(x)
    return out


def substitute(inverse, lower, right):
    xs = []
    for i, inv in enumerate(inverse):
        r = right[i * BLK : (i + 1) * BLK]
        if i:
            r = r - dot_exact_left(lower(i, i), jnp.concatenate(xs, axis=0))
        xs.append(dot3(inv, r))
    return jnp.concatenate(xs, axis=0)


def first_kernel(where_ref, own_ref, other_ref, recip_ref, right_ref, panel_ref, inv_ref, x_ref, cols_ref):
    c, which = where_ref[0], where_ref[1]
    groups, count, w, rows = own_ref.shape
    width = groups * 2 * w
    for k in range(count):
        for g in range(groups):
            cols_ref[k, g, c] = own_ref[g, k]
            cols_ref[k, g, 1 - c] = other_ref[g, k]
        panel_ref[k] = cols_ref[k].reshape(width, rows).T
    low = [
        panel_ref[which, i * BLK : (i + 1) * BLK, i * BLK : (i + 1) * BLK].astype(F32) for i in range(width // BLK)
    ]
    inverse = invert_blocks(low, recip_ref[which])
    for i, inv in enumerate(inverse):
        inv_ref[i] = inv
    x_ref[...] = substitute(
        inverse, lambda i, j: panel_ref[which, i * BLK : (i + 1) * BLK, : j * BLK], right_ref[...]
    )


def second_kernel(where_ref, panel_ref, inv_ref, x0_ref, x_ref, right_ref, out_ref):
    count = inv_ref.shape[0]
    right = right_ref[...] - dot_exact_left(panel_ref[0], x0_ref[...])
    inverse = [inv_ref[i] for i in range(count)]
    x1 = substitute(inverse, lambda i, j: panel_ref[1, i * BLK : (i + 1) * BLK, : j * BLK], right)
    out_ref[...] = jnp.where(where_ref[1] == 1, x1, x_ref[...])


def last_kernel(where_ref, panel_ref, pieces_ref, x_ref, right_ref, out_ref):
    count = panel_ref.shape[0]
    width = panel_ref.shape[2]
    total = right_ref[...]
    for k in range(count):
        x = pieces_ref[:, k].reshape(width, total.shape[1])
        total = total - dot_exact_left(panel_ref[k], x)
    out_ref[...] = jnp.where(where_ref[2] < count, x_ref[...], total)


def on_chip(kernel, out_shape, n_in, scratch=()):
    vmem = pl.BlockSpec(memory_space=pltpu.VMEM)
    return pl.pallas_call(
        kernel,
        out_shape=out_shape,
        in_specs=[pl.BlockSpec(memory_space=pltpu.SMEM)] + [vmem] * (n_in - 1),
        out_specs=jax.tree.map(lambda _: vmem, out_shape),
        scratch_shapes=list(scratch),
    )


def same_to_all(piece, axes):
    count = lax.axis_size(axes)
    return lax.all_to_all(jnp.broadcast_to(piece[None], (count, *piece.shape)), axes, 0, 0, tiled=True)


def body(factor, pivots, right):
    count, rows, w = factor.shape
    width = pivots.shape[1]
    columns = right.shape[1]
    me = lax.axis_index(ROW)
    core = lax.axis_index("c")
    where = jnp.stack([core, (me == 1).astype(jnp.int32), me]).astype(jnp.int32)
    recip = (1.0 / pivots).reshape(count, width // BLK, BLK // BASE, BASE)
    recip = jnp.repeat(jnp.swapaxes(recip, 2, 3), BASE, axis=3)

    piece = jnp.swapaxes(factor, 1, 2)
    near = same_to_all(piece, "zl")
    own = same_to_all(near, "x")
    own = own.reshape(-1, count, w, rows)
    other = lax.ppermute(own, "c", [(0, 1), (1, 0)])

    panel, inv, x = on_chip(
        first_kernel,
        (
            jax.ShapeDtypeStruct((count, rows, width), BF16),
            jax.ShapeDtypeStruct((width // BLK, BLK, BLK), F32),
            jax.ShapeDtypeStruct((rows, columns), F32),
        ),
        5,
        [pltpu.VMEM((count, own.shape[0], 2, w, rows), BF16)],
    )(where, own, other, recip, right)
    x0 = lax.ppermute(x, "y", [(0, 1)])
    out = jax.ShapeDtypeStruct((rows, columns), F32)
    x = on_chip(second_kernel, out, 6)(where, panel, inv, x0, x, right)
    n = lax.axis_size(ROW)
    mine = lax.all_to_all(x.reshape(n, rows // n, columns), ROW, 0, 0, tiled=True)[:count]
    pieces = same_to_all(mine, ROW)
    return on_chip(last_kernel, out, 5)(where, panel, pieces, x, right)


def solution(mesh):
    ids = mesh.devices
    shape = (2, ids.shape[0] // 2, ids.shape[1] // 8, 4, 2)
    split = Mesh(ids.reshape(shape), ROW + RHS)
    return jax.shard_map(
        body,
        mesh=split,
        in_specs=(P(None, ROW, RHS), P(), P(ROW, RHS)),
        out_specs=P(ROW, RHS),
        check_vma=False,
    )
```

time: 371 us -> 102 us (0.27)
  the two profiles are of different devices: /device:TPU:2 before, /device:TPU:8 now
where the time goes in v1:
time: 102 us; the launch traced here: 101 us
  blocking collectives  71.1 us (70%)
  Pallas kernels  12.1 us (12%)
  waiting for transfers between devices  9.51 us (9%)
  local copies, waits for them, and re-layouts  4.53 us (4%)
  starting transfers between devices  3.19 us (3%)
    all_to_all x3, blocking collectives, same_to_all(): lax.all_to_all(jnp.broadcast_to(piece[None], (count, *piece.shape)), axes...  48.3 us
    all_to_all x1, blocking collectives, body(): lax.all_to_all(x.reshape(n, rows // n, columns), ROW, 0, 0, tiled=True)  22.7 us
    ppermute x1, waiting for transfers between devices, body(): x0 = lax.ppermute(x, 'y', [(0, 1)])  9.51 us
    pallas_call x1, Pallas kernels, body(): on_chip(first_kernel, (jax.ShapeDtypeStruct((count, rows, width), BF16),...  5.78 us
    pallas_call x1, Pallas kernels, body(): x = on_chip(second_kernel, out, 6)(where, panel, inv, x0, x, right)  3.68 us
    pallas_call x1, Pallas kernels, body(): return on_chip(last_kernel, out, 5)(where, panel, pieces, x, right)  2.66 us
    unnamed x8, local copies, waits for them, and re-layouts  2.19 us
  transfers between devices with their start and end apart: 2, of which 1 were waited for; matrix products, arithmetic and copies ran while one was open for 2% of the time, Pallas kernels for 0%

profile of v1, /device:TPU:8, one launch (start us, length us, event | category | flops | bytes accessed | tf_op | source)
XLA Modules:
  0.0 101.1 jit_solution(12991638754824548189)
XLA Ops:
  0.0 0.8 broadcast_in_dim.8
  0.8 13.1 %all_to_all.20 = bf16[4,2,16,512]{3,2,1,0:T(8,128)(2,1)S(1)} all-to-all(bf16[4,2,16,512]{3,2,1,0:T(8,128)(2,1)S(1)} %broadcast_in_dim.8), channel_id=1, replica_groups=mesh['zh'=2,'y'=8,'x'=4,'zl'=4,'c'=2] {'zl'}, dimensions={0} | all-to-all | bytes 262144 | tf_op jit(solution)/shard_map/all_to_all | solution.py:147
  14.0 12.2 %all_to_all.21 = bf16[4,4,2,16,512]{4,3,2,1,0:T(8,128)(2,1)S(1)} all-to-all(bf16[4,4,2,16,512]{4,3,2,1,0:T(8,128)(2,1)S(1)} %broadcast_in_dim.9), channel_id=1, replica_groups=mesh['zh'=2,'y'=8,'x'=4,'zl'=4,'c'=2] {'x'}, dimensions={0} | all-to-all | bytes 1048576 | tf_op jit(solution)/shard_map/all_to_all | solution.py:147
  26.1 0.0 copy-start
  26.1 1.9 %collective-permute-start = (bf16[16,2,16,512]{3,2,1,0:T(8,128)(2,1)S(1)}, bf16[16,2,16,512]{3,2,1,0:T(8,128)(2,1)S(1)}, u32[]{:S(2)}, u32[]{:S(2)}) collective-permute-start(bf16[16,2,16,512]{3,2,1,0:T(8,128)(2,1)S(1)} %bitcast.8), channel_id=1, source_target_pairs={{0,1},{1,0},{2,3},{3,2},{4,5},{5,4},{6,7},{7,6},{8,9},{9,8},{10,11... | collective-permute-start | bytes 1572872 | tf_op jit(solution)/shard_map/ppermute | solution.py:164
  28.1 0.0 copy-start.3
  28.1 0.7 copy-done.3
  28.8 0.1 reshape.16
  28.9 0.1 copy.4
  29.0 0.3 broadcast_in_dim.10
  29.3 0.9 reshape.17.recip_ref
  30.2 0.0 copy-done
  30.2 0.7 pad_add_fusion.where_ref
  30.9 0.0 collective-permute-done.other_ref
  30.9 0.0 copy-start.1
  30.9 0.8 copy-done.1
  31.7 5.8 %shard_map.37 = (bf16[2,512,512]{2,1,0:T(8,128)(2,1)}, f32[4,128,128]{2,1,0:T(8,128)}, f32[512,128]{1,0:T(8,128)}) custom-call(s32[3]{0:T(128)} %pad_add_fusion.where_ref, bf16[16,2,16,512]{3,2,1,0:T(8,128)(2,1)} %bitcast.9, bf16[16,2,16,512]{3,2,1,0:T(8,128)(2,1)} %copy-done.1, f32[2,4,32,128]{3,2,1,0:T(8,128)} %reshape.17.recip_ref, f32[512,128]{1,0:T(8,128)} %right_ref.5), custom_call_target="tpu_custom_call" | custom-call | tf_op jit(solution)/shard_map/pallas_call | solution.py:166
  37.5 1.3 %collective-permute-start.1 = (f32[512,128]{1,0:T(8,128)}, f32[512,128]{1,0:T(8,128)S(1)}, u32[]{:S(2)}, u32[]{:S(2)}) collective-permute-start(f32[512,128]{1,0:T(8,128)} %get-tuple-element.10.x_ref), channel_id=1, source_target_pairs={{0,32},{1,33},{2,34},{3,35},{4,36},{5,37},{6,38},{7,39},{8,40},{9,... | collective-permute-start | bytes 786440 | tf_op jit(solution)/shard_map/ppermute | solution.py:176
  38.8 9.5 %collective-permute-done.1.x0_ref = f32[512,128]{1,0:T(8,128)S(1)} collective-permute-done((f32[512,128]{1,0:T(8,128)}, f32[512,128]{1,0:T(8,128)S(1)}, u32[]{:S(2)}, u32[]{:S(2)}) %collective-permute-start.1) | collective-permute-done | bytes 262176 | tf_op jit(solution)/shard_map/ppermute | solution.py:176
  48.3 0.0 copy-start.2
  48.3 0.7 copy-done.2
  49.0 3.7 %shard_map.38.x_ref = f32[512,128]{1,0:T(8,128)} custom-call(s32[3]{0:T(128)} %pad_add_fusion.where_ref, bf16[2,512,512]{2,1,0:T(8,128)(2,1)} %get-tuple-element.8.panel_ref, f32[4,128,128]{2,1,0:T(8,128)} %get-tuple-element.9.inv_ref, f32[512,128]{1,0:T(8,128)} %copy-done.2, f32[512,128]{1,0:T(8,128)} %get-tuple-element.10.x_ref, f32[512,128]{1,0:T(8,128)} %right_ref.5), custom_call_target="tpu_custom_call" | custom-call | tf_op jit(solution)/shard_map/pallas_call | solution.py:178
  52.7 22.7 %all_to_all.22 = f32[16,32,128]{2,1,0:T(8,128)S(1)} all-to-all(f32[16,32,128]{2,1,0:T(8,128)} %bitcast.7), channel_id=1, replica_groups=mesh['zh'=2,'y'=8,'x'=4,'zl'=4,'c'=2] {'zh','y'}, dimensions={0} | all-to-all | bytes 524288 | tf_op jit(solution)/shard_map/all_to_all | solution.py:180
  75.4 0.1 broadcast_in_dim.11
  75.5 23.0 %all_to_all.23.pieces_ref = f32[16,2,32,128]{3,2,1,0:T(8,128)} all-to-all(f32[16,2,32,128]{3,2,1,0:T(8,128)S(1)} %broadcast_in_dim.11), channel_id=1, replica_groups=mesh['zh'=2,'y'=8,'x'=4,'zl'=4,'c'=2] {'zh','y'}, dimensions={0} | all-to-all | bytes 1048576 | tf_op jit(solution)/shard_map/all_to_all | solution.py:147
  98.5 2.7 %shard_map.39 = f32[512,128]{1,0:T(8,128)} custom-call(s32[3]{0:T(128)} %pad_add_fusion.where_ref, bf16[2,512,512]{2,1,0:T(8,128)(2,1)} %get-tuple-element.8.panel_ref, f32[16,2,32,128]{3,2,1,0:T(8,128)} %all_to_all.23.pieces_ref, f32[512,128]{1,0:T(8,128)} %shard_map.38.x_ref, f32[512,128]{1,0:T(8,128)} %right_ref.5), custom_call_target="tpu_custom_call" | custom-call | tf_op jit(solution)/shard_map/pallas_call | solution.py:182
  (3 shorter events, 0.1 us)
Async XLA Ops:
  26.1 4.1 %copy-start = (bf16[4,4,2,16,512]{4,3,2,1,0:T(8,128)(2,1)}, bf16[4,4,2,16,512]{4,3,2,1,0:T(8,128)(2,1)S(1)}, u32[]{:S(2)}) copy-start(bf16[4,4,2,16,512]{4,3,2,1,0:T(8,128)(2,1)S(1)} %all_to_all.21) | copy-start | bytes 1572868
  26.1 4.8 %collective-permute-start = (bf16[16,2,16,512]{3,2,1,0:T(8,128)(2,1)S(1)}, bf16[16,2,16,512]{3,2,1,0:T(8,128)(2,1)S(1)}, u32[]{:S(2)}, u32[]{:S(2)}) collective-permute-start(bf16[16,2,16,512]{3,2,1,0:T(8,128)(2,1)S(1)} %bitcast.8), channel_id=1, source_target_pairs={{0,1},{1,0},{2,3},{3,2},{4,5},{5,4},{6,7},{7,6},{8,9},{9,8},{10,11... | collective-permute-start | bytes 1572872 | tf_op jit(solution)/shard_map/ppermute | solution.py:164
  28.1 0.7 copy-start.3
  30.9 0.8 copy-start.1
  37.5 10.8 %collective-permute-start.1 = (f32[512,128]{1,0:T(8,128)}, f32[512,128]{1,0:T(8,128)S(1)}, u32[]{:S(2)}, u32[]{:S(2)}) collective-permute-start(f32[512,128]{1,0:T(8,128)} %get-tuple-element.10.x_ref), channel_id=1, source_target_pairs={{0,32},{1,33},{2,34},{3,35},{4,36},{5,37},{6,38},{7,39},{8,40},{9,... | collective-permute-start | bytes 786440 | tf_op jit(solution)/shard_map/ppermute | solution.py:176
  48.3 0.7 copy-start.2

commit v2 on v1

v2 whole, which is shorter than its diff:
```python
import jax
import jax.numpy as jnp
from jax import lax
from jax.experimental import pallas as pl
from jax.experimental.pallas import tpu as pltpu
from jax.sharding import Mesh
from jax.sharding import PartitionSpec as P


ROW = ("zh", "yh", "yl")
RHS = ("x", "zl", "c")
F32, BF16 = jnp.float32, jnp.bfloat16
BASE, BLK, BIG = 32, 128, 256
SPAN = 14.0


def split2(v):
    hi = v.astype(BF16)
    lo = (v - hi.astype(F32)).astype(BF16)
    return hi, lo


def mm(a, b, trans=False):
    return lax.dot_general(a, b, (((1,), (1 if trans else 0,)), ((), ())), preferred_element_type=F32)


def dot_exact_left(a, v):
    n = v.shape[1]
    both = mm(a, jnp.concatenate(split2(v), axis=1))
    return both[:, :n] + both[:, n:]


def dot_exact_right(v, b):
    m = v.shape[0]
    both = mm(jnp.concatenate(split2(v), axis=0), b)
    return both[:m] + both[m:]


def dot3(a, b, trans=False):
    m = a.shape[0]
    ah, al = split2(a)
    bh, bl = split2(b)
    both = mm(jnp.concatenate([ah, al], axis=0), bh, trans)
    return both[:m] + (both[m:] + mm(ah, bl, trans))


def iota(shape, dim):
    return lax.broadcasted_iota(jnp.int32, shape, dim)


def spread_recip(pivot, row, seg):
    lane = iota((BASE, BLK), 1)
    left = jnp.where(lane % BASE == iota((BASE, BLK), 0), pivot, 0.0)
    same = jnp.where(row // BASE == seg, 1.0, 0.0).astype(BF16)
    a, rest = split2(left)
    b = rest
    c = (left - a.astype(F32) - b.astype(F32)).astype(BF16)
    got = mm(jnp.concatenate([a, b, c], axis=0), same)
    return 1.0 / (got[:BASE] + got[BASE : 2 * BASE] + got[2 * BASE :])


def invert_blocks(low, pivot):
    count = len(low)
    row, lane = iota((BLK, BLK), 0), iota((BLK, BLK), 1)
    seg = lane // BASE
    recip = [spread_recip(p, row, seg) for p in pivot]
    packed = []
    for blk in low:
        strict = jnp.where(row > lane, blk, 0.0)
        part = strict[:BASE]
        for s in range(1, BLK // BASE):
            part = jnp.where(seg[:BASE] == s, strict[s * BASE : (s + 1) * BASE], part)
        packed.append(part)
    packed = jnp.concatenate(packed, axis=0).astype(BF16)
    pick = row - seg * BASE
    one = jnp.where(row[:BASE] == lane[:BASE] % BASE, 1.0, 0.0).astype(F32)
    r = [one] * count
    for i in range(BASE - 1):
        spread = mm(packed, jnp.where(pick == i, 1.0, 0.0).astype(BF16))
        top = (i + 1) // 8 * 8
        for k in range(count):
            x = r[k][i : i + 1] * recip[k][i : i + 1]
            tail = r[k][top:] - spread[k * BASE + top : (k + 1) * BASE] * x
            r[k] = jnp.concatenate([r[k][:top], tail], axis=0) if top else tail
    out = []
    for k in range(count):
        x = r[k] * recip[k]
        out.append(jnp.where(row // BASE == seg, jnp.concatenate([x] * (BLK // BASE), axis=0), 0.0))
    size = BASE
    while size < BLK:
        off = (row // size > lane // size) & (row // (2 * size) == lane // (2 * size))
        half = [dot_exact_right(x, jnp.where(off, blk, 0.0).astype(BF16)) for x, blk in zip(out, low)]
        out = [x - dot3(h, x) for x, h in zip(out, half)]
        size *= 2
    return out


def join_blocks(first, second, low):
    off = -dot3(second, dot_exact_left(low, first))
    top = jnp.concatenate([first, jnp.zeros_like(first)], axis=1)
    return jnp.concatenate([top, jnp.concatenate([off, second], axis=1)], axis=0)


def substitute(inverse, upper, right):
    xs = []
    for j, inv in enumerate(inverse):
        r = right[:, j * BIG : (j + 1) * BIG]
        if j:
            r = r - dot_exact_right(jnp.concatenate(xs, axis=1), upper(j * BIG, j))
        xs.append(dot3(r, inv, trans=True))
    return jnp.concatenate(xs, axis=1)


def scaled(x):
    largest = jnp.max(jnp.abs(x), axis=1, keepdims=True)
    power = jnp.clip(jnp.ceil(jnp.log2(largest)), -100.0, 127.0)
    return jnp.concatenate([x * jnp.exp2(SPAN - power), jnp.broadcast_to(power, (x.shape[0], BLK))], axis=1)


def solve_kernel(
    where_ref, own_ref, other_ref, pivot_ref, first_ref, right_ref, x_ref, sent_ref, panel_ref, top_ref
):
    me, core = where_ref[0], where_ref[1]
    groups, panels, w, _ = own_ref.shape
    for k in range(panels):
        into = top_ref if k == panels - 1 else panel_ref.at[k]
        for g in range(groups):
            into[pl.ds(pl.multiple_of((2 * g + core) * w, w), w)] = own_ref[g, k]
            into[pl.ds(pl.multiple_of((2 * g + 1 - core) * w, w), w)] = other_ref[g, k]
    width = 2 * groups * w
    blocks = width // BLK
    low, pivot = [], []
    for k, ref in enumerate((top_ref, panel_ref.at[1])):
        for i in range(blocks):
            s = slice(i * BLK, (i + 1) * BLK)
            low.append(ref[s, s].astype(F32).T)
            pivot.append(pivot_ref[k : k + 1, s])
    small = invert_blocks(low, pivot)
    inverse = []
    for k, ref in enumerate((top_ref, panel_ref.at[1])):
        for i in range(0, blocks, 2):
            at = i * BLK
            sub = ref[at : at + BLK, at + BLK : at + 2 * BLK].astype(F32).T.astype(BF16)
            inverse.append(join_blocks(small[k * blocks + i], small[k * blocks + i + 1], sub))
    half = len(inverse) // 2
    right = right_ref[...].T
    b0 = jnp.where(me == 0, right, first_ref[...].T)
    x0 = substitute(inverse[:half], lambda n, j: top_ref[:n, j * BIG : (j + 1) * BIG], b0)
    r1 = right - dot_exact_right(x0, panel_ref[0])
    x1 = substitute(inverse[half:], lambda n, j: panel_ref[1, :n, j * BIG : (j + 1) * BIG], r1)
    x = jnp.where(me == 0, x0, x1)
    x_ref[...] = x
    sent_ref[...] = scaled(x)


def last_kernel(where_ref, panel_ref, pieces_ref, x_ref, right_ref, out_ref):
    count, width, _ = panel_ref.shape
    columns = x_ref.shape[0]
    update = 0.0
    for k in range(count):
        got = pieces_ref[:, k].reshape(columns, width + BLK)
        term = dot_exact_right(got[:, :width], panel_ref[k])
        update = update + term * jnp.exp2(got[:, width : width + 1] - SPAN)
    solved = where_ref[0] < count
    turned = jnp.where(solved, x_ref[...], update).T
    out_ref[...] = jnp.where(solved, turned, right_ref[...] - turned)


def on_chip(kernel, out_shape, n_in, scratch=()):
    vmem = pl.BlockSpec(memory_space=pltpu.VMEM)
    return pl.pallas_call(
        kernel,
        out_shape=out_shape,
        in_specs=[pl.BlockSpec(memory_space=pltpu.SMEM)] + [vmem] * (n_in - 1),
        out_specs=jax.tree.map(lambda _: vmem, out_shape),
        scratch_shapes=list(scratch),
        compiler_params=pltpu.CompilerParams(vmem_limit_bytes=24 * 1024 * 1024),
    )


def same_to_all(piece, axes):
    count = lax.axis_size(axes)
    return lax.all_to_all(jnp.broadcast_to(piece[None], (count, *piece.shape)), axes, 0, 0, tiled=True)


def whole(factor, pivots, right):
    count, rows, w = factor.shape
    width = pivots.shape[1]
    columns = right.shape[1]
    where = jnp.stack([lax.axis_index(ROW), lax.axis_index("c")]).astype(jnp.int32)
    n = lax.axis_size(ROW)

    piece = jnp.swapaxes(factor, 1, 2)
    both = same_to_all(piece, ("yl", "zl"))
    both = both.reshape(2, -1, count, w, rows)
    first = lax.ppermute(right, "yl", [(0, 1)])
    own = jnp.where(lax.axis_index("yl") == 0, both[0], both[1])
    cols = jnp.concatenate([own, both[0][:, :1]], axis=1)
    cols = lax.all_gather(cols, "x", axis=0, tiled=True)
    other = lax.ppermute(cols, "c", [(0, 1), (1, 0)])

    x, sent, panel = on_chip(
        solve_kernel,
        (
            jax.ShapeDtypeStruct((columns, width), F32),
            jax.ShapeDtypeStruct((columns, width + BLK), F32),
            jax.ShapeDtypeStruct((count, width, rows), BF16),
        ),
        6,
        [pltpu.VMEM((width, rows), BF16)],
    )(where, cols, other, pivots, first, right)
    sent = sent.astype(jnp.float16).reshape(n, columns // n, width + BLK)
    mine = lax.all_to_all(sent, ROW, 0, 0, tiled=True)[:count]
    pieces = same_to_all(mine, ROW).astype(F32)
    return on_chip(last_kernel, jax.ShapeDtypeStruct((rows, columns), F32), 5)(where, panel, pieces, x, right)


def solution(mesh):
    ids = mesh.devices
    shape = (2, ids.shape[0] // 4, 2, ids.shape[1] // 8, 4, 2)
    split = Mesh(ids.reshape(shape), ROW + RHS)
    return jax.shard_map(
        whole,
        mesh=split,
        in_specs=(P(None, ROW, RHS), P(), P(ROW, RHS)),
        out_specs=P(ROW, RHS),
        check_vma=False,
    )
```

time: 102 us -> 94.6 us (0.927)
  blocking collectives: 71.1 us -> 57.2 us
  starting transfers between devices: 3.19 us -> 12.3 us
  waiting for transfers between devices: 9.51 us -> 17.1 us
  Pallas kernels: 12.1 us -> 5.79 us
  local copies, waits for them, and re-layouts: 4.53 us -> 1.54 us
    all_to_all x3 -> x1, blocking collectives: 48.3 us -> 18.2 us  [same_to_all(): lax.all_to_all(jnp.broadcast_to(piece[None], (count, *piece.shape)), axes...]
    all_gather x0 -> x1, blocking collectives: none -> 14.4 us  [whole(): cols = lax.all_gather(cols, 'x', axis=0, tiled=True)]
    all_to_all x0 -> x1, starting transfers between devices: none -> 9.13 us  [same_to_all(): lax.all_to_all(jnp.broadcast_to(piece[None], (count, *piece.shape)), axes...]
    all_to_all x0 -> x1, waiting for transfers between devices: none -> 7.9 us  [same_to_all(): lax.all_to_all(jnp.broadcast_to(piece[None], (count, *piece.shape)), axes...]
    pallas_call x3 -> x2, Pallas kernels: 12.1 us -> 5.79 us  [the longest x1 3.99 us: whole(): on_chip(solve_kernel, (jax.ShapeDtypeStruct((columns, width), F32), jax.S...]
    unnamed x8 -> x4, local copies, waits for them, and re-layouts: 2.19 us -> 0.01 us
    all_to_all x1, blocking collectives: 22.7 us -> 24.6 us  [whole(): mine = lax.all_to_all(sent, ROW, 0, 0, tiled=True)[:count]]
  transfers between devices with their start and end apart: 2 -> 3, of which waited for: 1 -> 2; matrix products, arithmetic and copies ran while one was open for 2% -> 0% of each run, Pallas kernels for 0% -> 0%
where the time goes in v2:
time: 94.6 us; the launch traced here: 94.2 us
  blocking collectives  57.2 us (60%)
  waiting for transfers between devices  17.1 us (18%)
  starting transfers between devices  12.3 us (13%)
  Pallas kernels  5.79 us (6%)
  local copies, waits for them, and re-layouts  1.54 us (2%)
    all_to_all x1, blocking collectives, whole(): mine = lax.all_to_all(sent, ROW, 0, 0, tiled=True)[:count]  24.6 us
    all_to_all x1, blocking collectives, same_to_all(): lax.all_to_all(jnp.broadcast_to(piece[None], (count, *piece.shape)), axes...  18.2 us
    all_gather x1, blocking collectives, whole(): cols = lax.all_gather(cols, 'x', axis=0, tiled=True)  14.4 us
    ppermute x1, waiting for transfers between devices, whole(): first = lax.ppermute(right, 'yl', [(0, 1)])  9.2 us
    all_to_all x1, starting transfers between devices, same_to_all(): lax.all_to_all(jnp.broadcast_to(piece[None], (count, *piece.shape)), axes...  9.13 us
    all_to_all x1, waiting for transfers between devices, same_to_all(): lax.all_to_all(jnp.broadcast_to(piece[None], (count, *piece.shape)), axes...  7.9 us
    pallas_call x1, Pallas kernels, whole(): on_chip(solve_kernel, (jax.ShapeDtypeStruct((columns, width), F32), jax.S...  3.99 us
    ppermute x1, starting transfers between devices, whole(): other = lax.ppermute(cols, 'c', [(0, 1), (1, 0)])  1.91 us
  transfers between devices with their start and end apart: 3, of which 2 were waited for; matrix products, arithmetic and copies ran while one was open for 0% of the time, Pallas kernels for 0%

profile of v2, /device:TPU:8, one launch (start us, length us, event | category | flops | bytes accessed | tf_op | source)
XLA Modules:
  0.0 94.2 jit_solution(2891611782307616933)
XLA Ops:
  0.0 1.5 %broadcast_in_dim.4 = bf16[8,2,16,512]{3,2,1,0:T(8,128)(2,1)} broadcast(bf16[2,16,512]{2,1,0:T(8,128)(2,1)} %bitcast.5), dimensions={1,2,3} | broadcast | bytes 294912 | tf_op jit(solution)/shard_map/broadcast_in_dim | solution.py:183
  1.5 9.1 %all-to-all-start = ((bf16[8,2,16,512]{3,2,1,0:T(8,128)(2,1)}), bf16[8,2,16,512]{3,2,1,0:T(8,128)(2,1)S(1)}, u32[]{:S(2)}, u32[]{:S(2)}) async-start(bf16[8,2,16,512]{3,2,1,0:T(8,128)(2,1)} %broadcast_in_dim.4), calls=%async_computation | async-start | bytes 524288 | tf_op jit(solution)/shard_map/all_to_all | solution.py:183
  10.6 7.9 %all-to-all-done = bf16[8,2,16,512]{3,2,1,0:T(8,128)(2,1)S(1)} async-done(((bf16[8,2,16,512]{3,2,1,0:T(8,128)(2,1)}), bf16[8,2,16,512]{3,2,1,0:T(8,128)(2,1)S(1)}, u32[]{:S(2)}, u32[]{:S(2)}) %all-to-all-start) | async-done | bytes 262176 | tf_op jit(solution)/shard_map/all_to_all | solution.py:183
  18.6 0.0 copy-start
  18.6 14.4 %all_gather.3.own_ref = bf16[16,3,16,512]{3,2,1,0:T(8,128)(2,1)S(1)} all-gather(bf16[4,3,16,512]{3,2,1,0:T(8,128)(2,1)S(1)} %pad_maximum_fusion), channel_id=1, replica_groups=mesh['zh'=2,'yh'=4,'yl'=2,'x'=4,'zl'=4,'c'=2] {'x'}, dimensions={0}, use_global_device_ids=true | all-gather | bytes 983040 | tf_op jit(solution)/shard_map/all_gather | solution.py:199
  33.0 1.9 %collective-permute-start = (bf16[16,3,16,512]{3,2,1,0:T(8,128)(2,1)S(1)}, bf16[16,3,16,512]{3,2,1,0:T(8,128)(2,1)S(1)}, u32[]{:S(2)}, u32[]{:S(2)}) collective-permute-start(bf16[16,3,16,512]{3,2,1,0:T(8,128)(2,1)S(1)} %all_gather.3.own_ref), channel_id=1, source_target_pairs={{0,1},{1,0},{2,3},{3,2},{4,5},{5,4},{6,7},{7,6},{8,9},{9,8},{10,11... | collective-permute-start | bytes 2359304 | tf_op jit(solution)/shard_map/ppermute | solution.py:200
  34.9 0.0 copy-done
  34.9 1.3 %collective-permute-start.1 = (f32[512,128]{1,0:T(8,128)S(1)}, f32[512,128]{1,0:T(8,128)S(1)}, u32[]{:S(2)}, u32[]{:S(2)}) collective-permute-start(f32[512,128]{1,0:T(8,128)S(1)} %copy-done), channel_id=1, source_target_pairs={{0,32},{1,33},{2,34},{3,35},{4,36},{5,37},{6,38},{7,39},{8,40},{9,... | collective-permute-start | bytes 786440 | tf_op jit(solution)/shard_map/ppermute | solution.py:196
  36.2 0.0 copy-start.1
  36.2 0.1 pad_add_fusion.where_ref
  36.3 9.2 %collective-permute-done.1.first_ref = f32[512,128]{1,0:T(8,128)S(1)} collective-permute-done((f32[512,128]{1,0:T(8,128)S(1)}, f32[512,128]{1,0:T(8,128)S(1)}, u32[]{:S(2)}, u32[]{:S(2)}) %collective-permute-start.1) | collective-permute-done | bytes 262176 | tf_op jit(solution)/shard_map/ppermute | solution.py:196
  45.5 0.0 collective-permute-done.other_ref
  45.5 0.0 copy-done.1
  45.5 4.0 %shard_map.37 = (f32[128,512]{1,0:T(8,128)S(1)}, f32[128,640]{1,0:T(8,128)S(1)}, bf16[2,512,512]{2,1,0:T(8,128)(2,1)S(1)}) custom-call(s32[2]{0:T(128)S(1)} %pad_add_fusion.where_ref, bf16[16,3,16,512]{3,2,1,0:T(8,128)(2,1)S(1)} %all_gather.3.own_ref, bf16[16,3,16,512]{3,2,1,0:T(8,128)(2,1)S(1)} %collective-permute-done.other_ref, f32[2,512]{1,0:T(2,128)S(1)} %copy-done.1, ...), custom_call_target="tpu_custom_call" | custom-call | tf_op jit(solution)/shard_map/pallas_call | solution.py:202
  49.5 24.6 %all_to_all.15 = f16[16,8,640]{2,1,0:T(8,128)(2,1)S(1)} all-to-all(f16[16,8,640]{2,1,0:T(8,128)(2,1)S(1)} %convert_bitcast_fusion), channel_id=1, replica_groups=mesh['zh'=2,'yh'=4,'yl'=2,'x'=4,'zl'=4,'c'=2] {'zh','yh','yl'}, dimensions={0} | all-to-all | bytes 327680 | tf_op jit(solution)/shard_map/all_to_all | solution.py:213
  74.2 18.2 %all_to_all.16 = f16[16,2,8,640]{3,2,1,0:T(8,128)(2,1)S(1)} all-to-all(f16[16,2,8,640]{3,2,1,0:T(8,128)(2,1)S(1)} %broadcast_in_dim.5), channel_id=1, replica_groups=mesh['zh'=2,'yh'=4,'yl'=2,'x'=4,'zl'=4,'c'=2] {'zh','yh','yl'}, dimensions={0} | all-to-all | bytes 655360 | tf_op jit(solution)/shard_map/all_to_all | solution.py:183
  92.4 1.8 %shard_map.38 = f32[512,128]{1,0:T(8,128)} custom-call(s32[2]{0:T(128)S(1)} %pad_add_fusion.where_ref, bf16[2,512,512]{2,1,0:T(8,128)(2,1)S(1)} %get-tuple-element.8.panel_ref, f32[16,2,8,640]{3,2,1,0:T(8,128)S(1)} %convert_element_type.7.pieces_ref, f32[128,512]{1,0:T(8,128)S(1)} %get-tuple-element.10.x_ref, f32[512,128]{1,0:T(8,128)S(1)} %copy-done), custom_call_target="tpu_custom_call" | custom-call | tf_op jit(solution)/shard_map/pallas_call | solution.py:215
  (7 shorter events, 0.1 us)
Async XLA Ops:
  1.5 17.0 %all-to-all-start = ((bf16[8,2,16,512]{3,2,1,0:T(8,128)(2,1)}), bf16[8,2,16,512]{3,2,1,0:T(8,128)(2,1)S(1)}, u32[]{:S(2)}, u32[]{:S(2)}) async-start(bf16[8,2,16,512]{3,2,1,0:T(8,128)(2,1)} %broadcast_in_dim.4), calls=%async_computation | async-start | bytes 524288 | tf_op jit(solution)/shard_map/all_to_all | solution.py:183
  18.6 16.3 %copy-start = (f32[512,128]{1,0:T(8,128)S(1)}, f32[512,128]{1,0:T(8,128)}, u32[]{:S(2)}) copy-start(f32[512,128]{1,0:T(8,128)} %right_ref.3) | copy-start | bytes 786436
  33.0 12.5 %collective-permute-start = (bf16[16,3,16,512]{3,2,1,0:T(8,128)(2,1)S(1)}, bf16[16,3,16,512]{3,2,1,0:T(8,128)(2,1)S(1)}, u32[]{:S(2)}, u32[]{:S(2)}) collective-permute-start(bf16[16,3,16,512]{3,2,1,0:T(8,128)(2,1)S(1)} %all_gather.3.own_ref), channel_id=1, source_target_pairs={{0,1},{1,0},{2,3},{3,2},{4,5},{5,4},{6,7},{7,6},{8,9},{9,8},{10,11... | collective-permute-start | bytes 2359304 | tf_op jit(solution)/shard_map/ppermute | solution.py:200
  34.9 10.6 %collective-permute-start.1 = (f32[512,128]{1,0:T(8,128)S(1)}, f32[512,128]{1,0:T(8,128)S(1)}, u32[]{:S(2)}, u32[]{:S(2)}) collective-permute-start(f32[512,128]{1,0:T(8,128)S(1)} %copy-done), channel_id=1, source_target_pairs={{0,32},{1,33},{2,34},{3,35},{4,36},{5,37},{6,38},{7,39},{8,40},{9,... | collective-permute-start | bytes 786440 | tf_op jit(solution)/shard_map/ppermute | solution.py:196
  36.2 9.3 %copy-start.1 = (f32[2,512]{1,0:T(2,128)S(1)}, f32[2,512]{1,0:T(2,128)}, u32[]{:S(2)}) copy-start(f32[2,512]{1,0:T(2,128)} %pivot_ref.1) | copy-start | bytes 12292

commit v3 on v2

--- a/solution.py
+++ b/solution.py
@@ -5,7 +5,6 @@
 from jax.experimental.pallas import tpu as pltpu
 from jax.sharding import Mesh
 from jax.sharding import PartitionSpec as P
-
 
 ROW = ("zh", "yh", "yl")
 RHS = ("x", "zl", "c")
@@ -117,40 +116,54 @@
     return jnp.concatenate([x * jnp.exp2(SPAN - power), jnp.broadcast_to(power, (x.shape[0], BLK))], axis=1)
 
 
-def solve_kernel(
-    where_ref, own_ref, other_ref, pivot_ref, first_ref, right_ref, x_ref, sent_ref, panel_ref, top_ref
-):
+def first_kernel(where_ref, own_ref, other_ref, pivot_ref, right_ref, x_ref, sent_ref, inv_ref, panel_ref):
     me, core = where_ref[0], where_ref[1]
-    groups, panels, w, _ = own_ref.shape
-    for k in range(panels):
-        into = top_ref if k == panels - 1 else panel_ref.at[k]
+    groups, count, w, rows = own_ref.shape
+    for k in range(count):
+        into = panel_ref.at[k]
         for g in range(groups):
             into[pl.ds(pl.multiple_of((2 * g + core) * w, w), w)] = own_ref[g, k]
             into[pl.ds(pl.multiple_of((2 * g + 1 - core) * w, w), w)] = other_ref[g, k]
-    width = 2 * groups * w
-    blocks = width // BLK
-    low, pivot = [], []
-    for k, ref in enumerate((top_ref, panel_ref.at[1])):
+
+    @pl.when(me < count)
+    def _():
+        blocks = 2 * groups * w // BLK
+        low, pivot = [], []
         for i in range(blocks):
             s = slice(i * BLK, (i + 1) * BLK)
-            low.append(ref[s, s].astype(F32).T)
-            pivot.append(pivot_ref[k : k + 1, s])
-    small = invert_blocks(low, pivot)
-    inverse = []
-    for k, ref in enumerate((top_ref, panel_ref.at[1])):
+            low.append(panel_ref[me, s, s].astype(F32).T)
+            pivot.append(jnp.where(me == 0, pivot_ref[0:1, s], pivot_ref[1:2, s]))
+        small = invert_blocks(low, pivot)
+        inverse = []
         for i in range(0, blocks, 2):
             at = i * BLK
-            sub = ref[at : at + BLK, at + BLK : at + 2 * BLK].astype(F32).T.astype(BF16)
-            inverse.append(join_blocks(small[k * blocks + i], small[k * blocks + i + 1], sub))
-    half = len(inverse) // 2
-    right = right_ref[...].T
-    b0 = jnp.where(me == 0, right, first_ref[...].T)
-    x0 = substitute(inverse[:half], lambda n, j: top_ref[:n, j * BIG : (j + 1) * BIG], b0)
-    r1 = right - dot_exact_right(x0, panel_ref[0])
-    x1 = substitute(inverse[half:], lambda n, j: panel_ref[1, :n, j * BIG : (j + 1) * BIG], r1)
-    x = jnp.where(me == 0, x0, x1)
-    x_ref[...] = x
-    sent_ref[...] = scaled(x)
+            sub = panel_ref[me, at : at + BLK, at + BLK : at + 2 * BLK].astype(F32).T.astype(BF16)
+            inverse.append(join_blocks(small[i], small[i + 1], sub))
+            inv_ref[i // 2] = inverse[-1]
+        x = substitute(inverse, lambda n, j: panel_ref[me, :n, j * BIG : (j + 1) * BIG], right_ref[...].T)
+        x_ref[...] = x
+        sent_ref[...] = scaled(x)
+
+
+def unscaled(got):
+    return got[:, :-BLK] * jnp.exp2(got[:, -BLK : 1 - BLK] - SPAN)
+
+
+def second_kernel(where_ref, got_ref, panel_ref, inv_ref, right_ref, x_ref, sent_ref, out_ref, out_sent_ref):
+    me = where_ref[0]
+
+    @pl.when(me == 0)
+    def _():
+        out_ref[...] = x_ref[...]
+        out_sent_ref[...] = sent_ref[...]
+
+    @pl.when(me == 1)
+    def _():
+        inverse = [inv_ref[i] for i in range(inv_ref.shape[0])]
+        right = right_ref[...].T - dot_exact_right(unscaled(got_ref[...]), panel_ref[0])
+        x = substitute(inverse, lambda n, j: panel_ref[1, :n, j * BIG : (j + 1) * BIG], right)
+        out_ref[...] = x
+        out_sent_ref[...] = scaled(x)
 
 
 def last_kernel(where_ref, panel_ref, pieces_ref, x_ref, right_ref, out_ref):
@@ -159,8 +172,7 @@
     update = 0.0
     for k in range(count):
         got = pieces_ref[:, k].reshape(columns, width + BLK)
-        term = dot_exact_right(got[:, :width], panel_ref[k])
-        update = update + term * jnp.exp2(got[:, width : width + 1] - SPAN)
+        update = update + dot_exact_right(unscaled(got), panel_ref[k])
     solved = where_ref[0] < count
     turned = jnp.where(solved, x_ref[...], update).T
     out_ref[...] = jnp.where(solved, turned, right_ref[...] - turned)
@@ -183,7 +195,7 @@
     return lax.all_to_all(jnp.broadcast_to(piece[None], (count, *piece.shape)), axes, 0, 0, tiled=True)
 
 
-def whole(factor, pivots, right):
+def body(factor, pivots, right):
     count, rows, w = factor.shape
     width = pivots.shape[1]
     columns = right.shape[1]
@@ -191,24 +203,14 @@
     n = lax.axis_size(ROW)
 
     piece = jnp.swapaxes(factor, 1, 2)
-    both = same_to_all(piece, ("yl", "zl"))
-    both = both.reshape(2, -1, count, w, rows)
-    first = lax.ppermute(right, "yl", [(0, 1)])
-    own = jnp.where(lax.axis_index("yl") == 0, both[0], both[1])
-    cols = jnp.concatenate([own, both[0][:, :1]], axis=1)
-    cols = lax.all_gather(cols, "x", axis=0, tiled=True)
-    other = lax.ppermute(cols, "c", [(0, 1), (1, 0)])
-
-    x, sent, panel = on_chip(
-        solve_kernel,
-        (
-            jax.ShapeDtypeStruct((columns, width), F32),
-            jax.ShapeDtypeStruct((columns, width + BLK), F32),
-            jax.ShapeDtypeStruct((count, width, rows), BF16),
-        ),
-        6,
-        [pltpu.VMEM((width, rows), BF16)],
-    )(where, cols, other, pivots, first, right)
+    own = same_to_all(same_to_all(piece, "zl"), "x").reshape(-1, count, w, rows)
+    other = lax.ppermute(own, "c", [(0, 1), (1, 0)])
+
+    solved = (jax.ShapeDtypeStruct((columns, width), F32), jax.ShapeDtypeStruct((columns, width + BLK), F32))
+    kept = (jax.ShapeDtypeStruct((width // BIG, BIG, BIG), F32), jax.ShapeDtypeStruct((count, width, rows), BF16))
+    x, sent, inverse, panel = on_chip(first_kernel, solved + kept, 5)(where, own, other, pivots, right)
+    got = lax.ppermute(sent.astype(jnp.float16), ROW, [(0, 1)]).astype(F32)
+    x, sent = on_chip(second_kernel, solved, 7)(where, got, panel, inverse, right, x, sent)
     sent = sent.astype(jnp.float16).reshape(n, columns // n, width + BLK)
     mine = lax.all_to_all(sent, ROW, 0, 0, tiled=True)[:count]
     pieces = same_to_all(mine, ROW).astype(F32)
@@ -220,7 +222,7 @@
     shape = (2, ids.shape[0] // 4, 2, ids.shape[1] // 8, 4, 2)
     split = Mesh(ids.reshape(shape), ROW + RHS)
     return jax.shard_map(
-        whole,
+        body,
         mesh=split,
         in_specs=(P(None, ROW, RHS), P(), P(ROW, RHS)),
         out_specs=P(ROW, RHS),

time: 94.6 us -> 78.3 us (0.83)
  starting transfers between devices: 12.3 us -> 3.2 us
  waiting for transfers between devices: 17.1 us -> 8.6 us
  blocking collectives: 57.2 us -> 58.8 us
    all_to_all x1 -> x3, blocking collectives: 18.2 us -> 43.5 us  [same_to_all(): lax.all_to_all(jnp.broadcast_to(piece[None], (count, *piece.shape)), axes...]
    all_gather x1 -> x0, blocking collectives: 14.4 us -> none  [whole(): cols = lax.all_gather(cols, 'x', axis=0, tiled=True)]
    all_to_all x1, blocking collectives: 24.6 us -> 15.3 us  [body(): mine = lax.all_to_all(sent, ROW, 0, 0, tiled=True)[:count]]
    all_to_all x1 -> x0, starting transfers between devices: 9.13 us -> none  [same_to_all(): lax.all_to_all(jnp.broadcast_to(piece[None], (count, *piece.shape)), axes...]
    all_to_all x1 -> x0, waiting for transfers between devices: 7.9 us -> none  [same_to_all(): lax.all_to_all(jnp.broadcast_to(piece[None], (count, *piece.shape)), axes...]
    pallas_call x2 -> x3, Pallas kernels: 5.79 us -> 6.2 us  [the longest x1 2.81 us: body(): on_chip(first_kernel, solved + kept, 5)(where, own, other, pivots, right)]
  transfers between devices with their start and end apart: 3 -> 2, of which waited for: 2 -> 2; matrix products, arithmetic and copies ran while one was open for 0% -> 0% of each run, Pallas kernels for 0% -> 0%
where the time goes in v3:
time: 78.3 us; the launch traced here: 77.9 us
  blocking collectives  58.8 us (75%)
  waiting for transfers between devices  8.6 us (11%)
  Pallas kernels  6.2 us (8%)
  starting transfers between devices  3.2 us (4%)
  local copies, waits for them, and re-layouts  0.87 us (1%)
    all_to_all x3, blocking collectives, same_to_all(): lax.all_to_all(jnp.broadcast_to(piece[None], (count, *piece.shape)), axes...  43.5 us
    all_to_all x1, blocking collectives, body(): mine = lax.all_to_all(sent, ROW, 0, 0, tiled=True)[:count]  15.3 us
    ppermute x1, waiting for transfers between devices, body(): got = lax.ppermute(sent.astype(jnp.float16), ROW, [(0, 1)]).astype(F32)  6.82 us
    pallas_call x1, Pallas kernels, body(): on_chip(first_kernel, solved + kept, 5)(where, own, other, pivots, right)  2.81 us
    ppermute x1, starting transfers between devices, body(): other = lax.ppermute(own, 'c', [(0, 1), (1, 0)])  1.91 us
    pallas_call x1, Pallas kernels, body(): on_chip(last_kernel, jax.ShapeDtypeStruct((rows, columns), F32), 5)  1.86 us
    ppermute x1, waiting for transfers between devices, body(): other = lax.ppermute(own, 'c', [(0, 1), (1, 0)])  1.78 us
  transfers between devices with their start and end apart: 2, of which 2 were waited for; matrix products, arithmetic and copies ran while one was open for 0% of the time, Pallas kernels for 0%

profile of v3, /device:TPU:8, one launch (start us, length us, event | category | flops | bytes accessed | tf_op | source)
XLA Modules:
  0.0 77.9 jit_solution(12431009874058779134)
XLA Ops:
  0.0 0.8 broadcast_in_dim.6
  0.8 13.1 %all_to_all.20 = bf16[4,2,16,512]{3,2,1,0:T(8,128)(2,1)S(1)} all-to-all(bf16[4,2,16,512]{3,2,1,0:T(8,128)(2,1)S(1)} %broadcast_in_dim.6), channel_id=1, replica_groups=mesh['zh'=2,'yh'=4,'yl'=2,'x'=4,'zl'=4,'c'=2] {'zl'}, dimensions={0} | all-to-all | bytes 262144 | tf_op jit(solution)/shard_map/all_to_all | solution.py:195
  14.0 0.0 copy-start
  14.0 12.3 %all_to_all.21 = bf16[4,4,2,16,512]{4,3,2,1,0:T(8,128)(2,1)S(1)} all-to-all(bf16[4,4,2,16,512]{4,3,2,1,0:T(8,128)(2,1)S(1)} %broadcast_in_dim.7), channel_id=1, replica_groups=mesh['zh'=2,'yh'=4,'yl'=2,'x'=4,'zl'=4,'c'=2] {'x'}, dimensions={0} | all-to-all | bytes 1048576 | tf_op jit(solution)/shard_map/all_to_all | solution.py:195
  26.3 1.9 %collective-permute-start = (bf16[16,2,16,512]{3,2,1,0:T(8,128)(2,1)S(1)}, bf16[16,2,16,512]{3,2,1,0:T(8,128)(2,1)S(1)}, u32[]{:S(2)}, u32[]{:S(2)}) collective-permute-start(bf16[16,2,16,512]{3,2,1,0:T(8,128)(2,1)S(1)} %bitcast.6), channel_id=1, source_target_pairs={{0,1},{1,0},{2,3},{3,2},{4,5},{5,4},{6,7},{7,6},{8,9},{9,8},{10,11... | collective-permute-start | bytes 1572872 | tf_op jit(solution)/shard_map/ppermute | solution.py:207
  28.2 0.0 copy-start.1
  28.2 0.1 pad_add_fusion.where_ref
  28.3 1.8 %collective-permute-done.other_ref = bf16[16,2,16,512]{3,2,1,0:T(8,128)(2,1)S(1)} collective-permute-done((bf16[16,2,16,512]{3,2,1,0:T(8,128)(2,1)S(1)}, bf16[16,2,16,512]{3,2,1,0:T(8,128)(2,1)S(1)}, u32[]{:S(2)}, u32[]{:S(2)}) %collective-permute-start) | collective-permute-done | bytes 524320 | tf_op jit(solution)/shard_map/ppermute | solution.py:207
  30.1 0.0 copy-done
  30.1 0.0 copy-done.1
  30.1 2.8 %shard_map.37 = (f32[128,512]{1,0:T(8,128)S(1)}, f32[128,640]{1,0:T(8,128)S(1)}, f32[2,256,256]{2,1,0:T(8,128)S(1)}, bf16[2,512,512]{2,1,0:T(8,128)(2,1)S(1)}) custom-call(s32[2]{0:T(128)S(1)} %pad_add_fusion.where_ref, bf16[16,2,16,512]{3,2,1,0:T(8,128)(2,1)S(1)} %bitcast.7, bf16[16,2,16,512]{3,2,1,0:T(8,128)(2,1)S(1)} %collective-permute-done.other_ref, ...), custom_call_target="tpu_custom_call" | custom-call | tf_op jit(solution)/shard_map/pallas_call | solution.py:211
  32.9 1.3 %collective-permute-start.1 = (f16[128,640]{1,0:T(8,128)(2,1)S(1)}, f16[128,640]{1,0:T(8,128)(2,1)S(1)}, u32[]{:S(2)}, u32[]{:S(2)}) collective-permute-start(f16[128,640]{1,0:T(8,128)(2,1)S(1)} %convert_element_type.12), channel_id=1, source_target_pairs={{0,32},{1,33},{2,34},{3,35},{4,36},{5,37},{6,38},{7,39},{8,40},{9,... | collective-permute-start | bytes 491528 | tf_op jit(solution)/shard_map/ppermute | solution.py:212
  34.2 6.8 %collective-permute-done.1 = f16[128,640]{1,0:T(8,128)(2,1)S(1)} collective-permute-done((f16[128,640]{1,0:T(8,128)(2,1)S(1)}, f16[128,640]{1,0:T(8,128)(2,1)S(1)}, u32[]{:S(2)}, u32[]{:S(2)}) %collective-permute-start.1) | collective-permute-done | bytes 163872 | tf_op jit(solution)/shard_map/ppermute | solution.py:212
  41.1 1.5 %shard_map.38 = (f32[128,512]{1,0:T(8,128)S(1)}, f32[128,640]{1,0:T(8,128)S(1)}) custom-call(s32[2]{0:T(128)S(1)} %pad_add_fusion.where_ref, f32[128,640]{1,0:T(8,128)S(1)} %convert_element_type.13.got_ref, bf16[2,512,512]{2,1,0:T(8,128)(2,1)S(1)} %get-tuple-element.11.panel_ref, f32[2,256,256]{2,1,0:T(8,128)S(1)} %get-tuple-element.13.inv_ref, ...), custom_call_target="tpu_custom_call" | custom-call | tf_op jit(solution)/shard_map/pallas_call | solution.py:213
  42.7 15.3 %all_to_all.22 = f16[16,8,640]{2,1,0:T(8,128)(2,1)S(1)} all-to-all(f16[16,8,640]{2,1,0:T(8,128)(2,1)S(1)} %convert_bitcast_fusion), channel_id=1, replica_groups=mesh['zh'=2,'yh'=4,'yl'=2,'x'=4,'zl'=4,'c'=2] {'zh','yh','yl'}, dimensions={0} | all-to-all | bytes 327680 | tf_op jit(solution)/shard_map/all_to_all | solution.py:215
  58.0 18.0 %all_to_all.23 = f16[16,2,8,640]{3,2,1,0:T(8,128)(2,1)S(1)} all-to-all(f16[16,2,8,640]{3,2,1,0:T(8,128)(2,1)S(1)} %broadcast_in_dim.8), channel_id=1, replica_groups=mesh['zh'=2,'yh'=4,'yl'=2,'x'=4,'zl'=4,'c'=2] {'zh','yh','yl'}, dimensions={0} | all-to-all | bytes 655360 | tf_op jit(solution)/shard_map/all_to_all | solution.py:195
  76.1 1.9 %shard_map.39 = f32[512,128]{1,0:T(8,128)} custom-call(s32[2]{0:T(128)S(1)} %pad_add_fusion.where_ref, bf16[2,512,512]{2,1,0:T(8,128)(2,1)S(1)} %get-tuple-element.11.panel_ref, f32[16,2,8,640]{3,2,1,0:T(8,128)S(1)} %convert_element_type.15.pieces_ref, f32[128,512]{1,0:T(8,128)S(1)} %get-tuple-element.16.x_ref, f32[512,128]{1,0:T(8,128)S(1)} %copy-done), custom_call_target="tpu_custom_call" | custom-call | tf_op jit(solution)/shard_map/pallas_call | solution.py:217
  (7 shorter events, 0.2 us)
Async XLA Ops:
  14.0 16.1 %copy-start = (f32[512,128]{1,0:T(8,128)S(1)}, f32[512,128]{1,0:T(8,128)}, u32[]{:S(2)}) copy-start(f32[512,128]{1,0:T(8,128)} %right_ref.5) | copy-start | bytes 786436
  26.3 3.8 %collective-permute-start = (bf16[16,2,16,512]{3,2,1,0:T(8,128)(2,1)S(1)}, bf16[16,2,16,512]{3,2,1,0:T(8,128)(2,1)S(1)}, u32[]{:S(2)}, u32[]{:S(2)}) collective-permute-start(bf16[16,2,16,512]{3,2,1,0:T(8,128)(2,1)S(1)} %bitcast.6), channel_id=1, source_target_pairs={{0,1},{1,0},{2,3},{3,2},{4,5},{5,4},{6,7},{7,6},{8,9},{9,8},{10,11... | collective-permute-start | bytes 1572872 | tf_op jit(solution)/shard_map/ppermute | solution.py:207
  28.2 1.9 %copy-start.1 = (f32[2,512]{1,0:T(2,128)S(1)}, f32[2,512]{1,0:T(2,128)}, u32[]{:S(2)}) copy-start(f32[2,512]{1,0:T(2,128)} %pivot_ref.1) | copy-start | bytes 12292
  32.9 8.1 %collective-permute-start.1 = (f16[128,640]{1,0:T(8,128)(2,1)S(1)}, f16[128,640]{1,0:T(8,128)(2,1)S(1)}, u32[]{:S(2)}, u32[]{:S(2)}) collective-permute-start(f16[128,640]{1,0:T(8,128)(2,1)S(1)} %convert_element_type.12), channel_id=1, source_target_pairs={{0,32},{1,33},{2,34},{3,35},{4,36},{5,37},{6,38},{7,39},{8,40},{9,... | collective-permute-start | bytes 491528 | tf_op jit(solution)/shard_map/ppermute | solution.py:212

commit v4 on v3

--- a/solution.py
+++ b/solution.py
@@ -5,6 +5,7 @@
 from jax.experimental.pallas import tpu as pltpu
 from jax.sharding import Mesh
 from jax.sharding import PartitionSpec as P
+
 
 ROW = ("zh", "yh", "yl")
 RHS = ("x", "zl", "c")
@@ -116,41 +117,47 @@
     return jnp.concatenate([x * jnp.exp2(SPAN - power), jnp.broadcast_to(power, (x.shape[0], BLK))], axis=1)
 
 
-def first_kernel(where_ref, own_ref, other_ref, pivot_ref, right_ref, x_ref, sent_ref, inv_ref, panel_ref):
-    me, core = where_ref[0], where_ref[1]
-    groups, count, w, rows = own_ref.shape
+def invert_panel(panel, pivot):
+    blocks = pivot.shape[1] // BLK
+    at = [slice(i * BLK, (i + 1) * BLK) for i in range(blocks)]
+    small = invert_blocks([panel[s, s].astype(F32).T for s in at], [pivot[:, s] for s in at])
+    return [
+        join_blocks(small[i], small[i + 1], panel[at[i], at[i + 1]].astype(F32).T.astype(BF16))
+        for i in range(0, blocks, 2)
+    ]
+
+
+def first_kernel(own_ref, other_ref, pivot_ref, right_ref, x_ref, sent_ref, panel_ref):
+    me, core = lax.axis_index(ROW), lax.axis_index("c")
+    groups, count, w, _ = own_ref.shape
     for k in range(count):
         into = panel_ref.at[k]
         for g in range(groups):
             into[pl.ds(pl.multiple_of((2 * g + core) * w, w), w)] = own_ref[g, k]
             into[pl.ds(pl.multiple_of((2 * g + 1 - core) * w, w), w)] = other_ref[g, k]
 
-    @pl.when(me < count)
-    def _():
-        blocks = 2 * groups * w // BLK
-        low, pivot = [], []
-        for i in range(blocks):
-            s = slice(i * BLK, (i + 1) * BLK)
-            low.append(panel_ref[me, s, s].astype(F32).T)
-            pivot.append(jnp.where(me == 0, pivot_ref[0:1, s], pivot_ref[1:2, s]))
-        small = invert_blocks(low, pivot)
-        inverse = []
-        for i in range(0, blocks, 2):
-            at = i * BLK
-            sub = panel_ref[me, at : at + BLK, at + BLK : at + 2 * BLK].astype(F32).T.astype(BF16)
-            inverse.append(join_blocks(small[i], small[i + 1], sub))
-            inv_ref[i // 2] = inverse[-1]
-        x = substitute(inverse, lambda n, j: panel_ref[me, :n, j * BIG : (j + 1) * BIG], right_ref[...].T)
+    @pl.when(me == 0)
+    def _():
+        inverse = invert_panel(panel_ref.at[0], pivot_ref[0:1])
+        x = substitute(inverse, lambda n, j: panel_ref[0, :n, j * BIG : (j + 1) * BIG], right_ref[...].T)
         x_ref[...] = x
         sent_ref[...] = scaled(x)
 
 
+def invert_kernel(panel_ref, pivot_ref, right_ref, inv_ref, turned_ref):
+    @pl.when(lax.axis_index(ROW) == 1)
+    def _():
+        turned_ref[...] = right_ref[...].T
+        for i, inv in enumerate(invert_panel(panel_ref.at[1], pivot_ref[1:2])):
+            inv_ref[i] = inv
+
+
 def unscaled(got):
     return got[:, :-BLK] * jnp.exp2(got[:, -BLK : 1 - BLK] - SPAN)
 
 
-def second_kernel(where_ref, got_ref, panel_ref, inv_ref, right_ref, x_ref, sent_ref, out_ref, out_sent_ref):
-    me = where_ref[0]
+def second_kernel(got_ref, panel_ref, inv_ref, turned_ref, x_ref, sent_ref, out_ref, out_sent_ref):
+    me = lax.axis_index(ROW)
 
     @pl.when(me == 0)
     def _():
@@ -160,20 +167,22 @@
     @pl.when(me == 1)
     def _():
         inverse = [inv_ref[i] for i in range(inv_ref.shape[0])]
-        right = right_ref[...].T - dot_exact_right(unscaled(got_ref[...]), panel_ref[0])
+        right = turned_ref[...] - dot_exact_right(unscaled(got_ref[...]), panel_ref[0])
         x = substitute(inverse, lambda n, j: panel_ref[1, :n, j * BIG : (j + 1) * BIG], right)
         out_ref[...] = x
         out_sent_ref[...] = scaled(x)
 
 
-def last_kernel(where_ref, panel_ref, pieces_ref, x_ref, right_ref, out_ref):
+def last_kernel(panel_ref, pieces_ref, x_ref, right_ref, out_ref):
     count, width, _ = panel_ref.shape
     columns = x_ref.shape[0]
+    got = pieces_ref[...].reshape(columns, count * width + BLK)
     update = 0.0
     for k in range(count):
-        got = pieces_ref[:, k].reshape(columns, width + BLK)
-        update = update + dot_exact_right(unscaled(got), panel_ref[k])
-    solved = where_ref[0] < count
+        at = count * width + k * BLK // count
+        x = got[:, k * width : (k + 1) * width] * jnp.exp2(got[:, at : at + 1] - SPAN)
+        update = update + dot_exact_right(x, panel_ref[k])
+    solved = lax.axis_index(ROW) < count
     turned = jnp.where(solved, x_ref[...], update).T
     out_ref[...] = jnp.where(solved, turned, right_ref[...] - turned)
 
@@ -183,7 +192,7 @@
     return pl.pallas_call(
         kernel,
         out_shape=out_shape,
-        in_specs=[pl.BlockSpec(memory_space=pltpu.SMEM)] + [vmem] * (n_in - 1),
+        in_specs=[vmem] * n_in,
         out_specs=jax.tree.map(lambda _: vmem, out_shape),
         scratch_shapes=list(scratch),
         compiler_params=pltpu.CompilerParams(vmem_limit_bytes=24 * 1024 * 1024),
@@ -195,11 +204,10 @@
     return lax.all_to_all(jnp.broadcast_to(piece[None], (count, *piece.shape)), axes, 0, 0, tiled=True)
 
 
-def body(factor, pivots, right):
+def whole(factor, pivots, right):
     count, rows, w = factor.shape
     width = pivots.shape[1]
     columns = right.shape[1]
-    where = jnp.stack([lax.axis_index(ROW), lax.axis_index("c")]).astype(jnp.int32)
     n = lax.axis_size(ROW)
 
     piece = jnp.swapaxes(factor, 1, 2)
@@ -207,14 +215,19 @@
     other = lax.ppermute(own, "c", [(0, 1), (1, 0)])
 
     solved = (jax.ShapeDtypeStruct((columns, width), F32), jax.ShapeDtypeStruct((columns, width + BLK), F32))
-    kept = (jax.ShapeDtypeStruct((width // BIG, BIG, BIG), F32), jax.ShapeDtypeStruct((count, width, rows), BF16))
-    x, sent, inverse, panel = on_chip(first_kernel, solved + kept, 5)(where, own, other, pivots, right)
-    got = lax.ppermute(sent.astype(jnp.float16), ROW, [(0, 1)]).astype(F32)
-    x, sent = on_chip(second_kernel, solved, 7)(where, got, panel, inverse, right, x, sent)
+    all_cols = (jax.ShapeDtypeStruct((count, width, rows), BF16),)
+    kept = (jax.ShapeDtypeStruct((width // BIG, BIG, BIG), F32), jax.ShapeDtypeStruct((columns, width), F32))
+    x, sent, panel = on_chip(first_kernel, solved + all_cols, 4)(own, other, pivots, right)
+    got = lax.ppermute(sent.astype(jnp.float16), ROW, [(0, 1)])
+    inverse, turned = on_chip(invert_kernel, kept, 3)(panel, pivots, right)
+    x, sent = on_chip(second_kernel, solved, 6)(got.astype(F32), panel, inverse, turned, x, sent)
     sent = sent.astype(jnp.float16).reshape(n, columns // n, width + BLK)
     mine = lax.all_to_all(sent, ROW, 0, 0, tiled=True)[:count]
+    share = BLK // count
+    power = [mine[k, :, width + k * share : width + (k + 1) * share] for k in range(count)]
+    mine = jnp.concatenate([mine[k, :, :width] for k in range(count)] + power, axis=1)
     pieces = same_to_all(mine, ROW).astype(F32)
-    return on_chip(last_kernel, jax.ShapeDtypeStruct((rows, columns), F32), 5)(where, panel, pieces, x, right)
+    return on_chip(last_kernel, jax.ShapeDtypeStruct((rows, columns), F32), 4)(panel, pieces, x, right)
 
 
 def solution(mesh):
@@ -222,7 +235,7 @@
     shape = (2, ids.shape[0] // 4, 2, ids.shape[1] // 8, 4, 2)
     split = Mesh(ids.reshape(shape), ROW + RHS)
     return jax.shard_map(
-        body,
+        whole,
         mesh=split,
         in_specs=(P(None, ROW, RHS), P(), P(ROW, RHS)),
         out_specs=P(ROW, RHS),

time: 78.3 us -> 76.8 us (0.981)
  Pallas kernels: 6.2 us -> 3.96 us
  blocking collectives: 58.8 us -> 60.7 us
  waiting for transfers between devices: 8.6 us -> 7.33 us
    pallas_call x3 -> x4, Pallas kernels: 6.2 us -> 3.96 us  [the longest x1 1.59 us: whole(): inverse, turned = on_chip(invert_kernel, kept, 3)(panel, pivots, right)]
    all_to_all x1, blocking collectives: 15.3 us -> 17.3 us  [whole(): mine = lax.all_to_all(sent, ROW, 0, 0, tiled=True)[:count]]
    ppermute x2, waiting for transfers between devices: 8.6 us -> 7.33 us  [the longest x1 5.46 us: whole(): got = lax.ppermute(sent.astype(jnp.float16), ROW, [(0, 1)])]
  transfers between devices with their start and end apart: 2 -> 2, of which waited for: 2 -> 2; matrix products, arithmetic and copies ran while one was open for 0% -> 0% of each run, Pallas kernels for 0% -> 2%
where the time goes in v4:
time: 76.8 us; the launch traced here: 76.4 us
  blocking collectives  60.7 us (79%)
  waiting for transfers between devices  7.33 us (10%)
  Pallas kernels  3.96 us (5%)
  starting transfers between devices  3.2 us (4%)
  local copies, waits for them, and re-layouts  1.03 us (1%)
    all_to_all x3, blocking collectives, same_to_all(): lax.all_to_all(jnp.broadcast_to(piece[None], (count, *piece.shape)), axes...  43.4 us
    all_to_all x1, blocking collectives, whole(): mine = lax.all_to_all(sent, ROW, 0, 0, tiled=True)[:count]  17.3 us
    ppermute x1, waiting for transfers between devices, whole(): got = lax.ppermute(sent.astype(jnp.float16), ROW, [(0, 1)])  5.46 us
    ppermute x1, starting transfers between devices, whole(): other = lax.ppermute(own, 'c', [(0, 1), (1, 0)])  1.91 us
    ppermute x1, waiting for transfers between devices, whole(): other = lax.ppermute(own, 'c', [(0, 1), (1, 0)])  1.88 us
    pallas_call x1, Pallas kernels, whole(): inverse, turned = on_chip(invert_kernel, kept, 3)(panel, pivots, right)  1.59 us
  transfers between devices with their start and end apart: 2, of which 2 were waited for; matrix products, arithmetic and copies ran while one was open for 0% of the time, Pallas kernels for 2%

profile of v4, /device:TPU:8, one launch (start us, length us, event | category | flops | bytes accessed | tf_op | source)
XLA Modules:
  0.0 76.4 jit_solution(15653783337514456682)
XLA Ops:
  0.0 0.8 %broadcast_in_dim.6 = bf16[4,2,16,512]{3,2,1,0:T(8,128)(2,1)S(1)} broadcast(bf16[2,16,512]{2,1,0:T(8,128)(2,1)} %bitcast.14), dimensions={1,2,3} | broadcast | bytes 163840 | tf_op jit(solution)/shard_map/broadcast_in_dim | solution.py:204
  0.8 13.1 %all_to_all.20 = bf16[4,2,16,512]{3,2,1,0:T(8,128)(2,1)S(1)} all-to-all(bf16[4,2,16,512]{3,2,1,0:T(8,128)(2,1)S(1)} %broadcast_in_dim.6), channel_id=1, replica_groups=mesh['zh'=2,'yh'=4,'yl'=2,'x'=4,'zl'=4,'c'=2] {'zl'}, dimensions={0} | all-to-all | bytes 262144 | tf_op jit(solution)/shard_map/all_to_all | solution.py:204
  14.0 0.0 copy-start
  14.0 0.0 copy-start.1
  14.0 12.3 %all_to_all.21 = bf16[4,4,2,16,512]{4,3,2,1,0:T(8,128)(2,1)S(1)} all-to-all(bf16[4,4,2,16,512]{4,3,2,1,0:T(8,128)(2,1)S(1)} %broadcast_in_dim.7), channel_id=1, replica_groups=mesh['zh'=2,'yh'=4,'yl'=2,'x'=4,'zl'=4,'c'=2] {'x'}, dimensions={0} | all-to-all | bytes 1048576 | tf_op jit(solution)/shard_map/all_to_all | solution.py:204
  26.3 1.9 %collective-permute-start = (bf16[16,2,16,512]{3,2,1,0:T(8,128)(2,1)S(1)}, bf16[16,2,16,512]{3,2,1,0:T(8,128)(2,1)S(1)}, u32[]{:S(2)}, u32[]{:S(2)}) collective-permute-start(bf16[16,2,16,512]{3,2,1,0:T(8,128)(2,1)S(1)} %bitcast.12), channel_id=1, source_target_pairs={{0,1},{1,0},{2,3},{3,2},{4,5},{5,4},{6,7},{7,6},{8,9},{9,8},{10,11... | collective-permute-start | bytes 1572872 | tf_op jit(solution)/shard_map/ppermute | solution.py:215
  28.2 1.9 %collective-permute-done.other_ref = bf16[16,2,16,512]{3,2,1,0:T(8,128)(2,1)S(1)} collective-permute-done((bf16[16,2,16,512]{3,2,1,0:T(8,128)(2,1)S(1)}, bf16[16,2,16,512]{3,2,1,0:T(8,128)(2,1)S(1)}, u32[]{:S(2)}, u32[]{:S(2)}) %collective-permute-start) | collective-permute-done | bytes 524320 | tf_op jit(solution)/shard_map/ppermute | solution.py:215
  30.1 0.0 copy-done
  30.1 0.0 copy-done.1
  30.1 0.1 shard_map.37
  30.2 1.3 %collective-permute-start.1 = (f16[128,640]{1,0:T(8,128)(2,1)S(1)}, f16[128,640]{1,0:T(8,128)(2,1)S(1)}, u32[]{:S(2)}, u32[]{:S(2)}) collective-permute-start(f16[128,640]{1,0:T(8,128)(2,1)S(1)} %convert_element_type.12), channel_id=1, source_target_pairs={{0,32},{1,33},{2,34},{3,35},{4,36},{5,37},{6,38},{7,39},{8,40},{9,... | collective-permute-start | bytes 491528 | tf_op jit(solution)/shard_map/ppermute | solution.py:221
  31.5 1.6 %shard_map.38 = (f32[2,256,256]{2,1,0:T(8,128)S(1)}, f32[128,512]{1,0:T(8,128)S(1)}) custom-call(bf16[2,512,512]{2,1,0:T(8,128)(2,1)S(1)} %get-tuple-element.12.panel_ref, f32[2,512]{1,0:T(2,128)S(1)} %copy-done.1, f32[512,128]{1,0:T(8,128)S(1)} %copy-done), custom_call_target="tpu_custom_call" | custom-call | tf_op jit(solution)/shard_map/pallas_call | solution.py:222
  33.1 5.5 %collective-permute-done.1 = f16[128,640]{1,0:T(8,128)(2,1)S(1)} collective-permute-done((f16[128,640]{1,0:T(8,128)(2,1)S(1)}, f16[128,640]{1,0:T(8,128)(2,1)S(1)}, u32[]{:S(2)}, u32[]{:S(2)}) %collective-permute-start.1) | collective-permute-done | bytes 163872 | tf_op jit(solution)/shard_map/ppermute | solution.py:221
  38.6 1.0 %shard_map.39 = (f32[128,512]{1,0:T(8,128)S(1)}, f32[128,640]{1,0:T(8,128)S(1)}) custom-call(f32[128,640]{1,0:T(8,128)S(1)} %convert_element_type.13.got_ref, bf16[2,512,512]{2,1,0:T(8,128)(2,1)S(1)} %get-tuple-element.12.panel_ref, f32[2,256,256]{2,1,0:T(8,128)S(1)} %get-tuple-element.14.inv_ref, f32[128,512]{1,0:T(8,128)S(1)} %get-tuple-element.15.turned_ref, ...), custom_call_target="tpu_custom_call" | custom-call | tf_op jit(solution)/shard_map/pallas_call | solution.py:223
  39.6 17.3 %all_to_all.22 = f16[16,8,640]{2,1,0:T(8,128)(2,1)S(1)} all-to-all(f16[16,8,640]{2,1,0:T(8,128)(2,1)S(1)} %convert_bitcast_fusion), channel_id=1, replica_groups=mesh['zh'=2,'yh'=4,'yl'=2,'x'=4,'zl'=4,'c'=2] {'zh','yh','yl'}, dimensions={0} | all-to-all | bytes 327680 | tf_op jit(solution)/shard_map/all_to_all | solution.py:225
  56.9 0.1 slice_bitcast_fusion.2
  57.0 0.1 concatenate.3
  57.1 18.0 %all_to_all.23 = f16[16,8,1152]{2,1,0:T(8,128)(2,1)S(1)} all-to-all(f16[16,8,1152]{2,1,0:T(8,128)(2,1)S(1)} %broadcast_in_dim.8), channel_id=1, replica_groups=mesh['zh'=2,'yh'=4,'yl'=2,'x'=4,'zl'=4,'c'=2] {'zh','yh','yl'}, dimensions={0} | all-to-all | bytes 589824 | tf_op jit(solution)/shard_map/all_to_all | solution.py:204
  75.1 1.3 %shard_map.40 = f32[512,128]{1,0:T(8,128)} custom-call(bf16[2,512,512]{2,1,0:T(8,128)(2,1)S(1)} %get-tuple-element.12.panel_ref, f32[16,8,1152]{2,1,0:T(8,128)S(1)} %convert_element_type.15.pieces_ref, f32[128,512]{1,0:T(8,128)S(1)} %get-tuple-element.18.x_ref, f32[512,128]{1,0:T(8,128)S(1)} %copy-done), custom_call_target="tpu_custom_call" | custom-call | tf_op jit(solution)/shard_map/pallas_call | solution.py:230
  (7 shorter events, 0.2 us)
Async XLA Ops:
  14.0 16.1 %copy-start = (f32[512,128]{1,0:T(8,128)S(1)}, f32[512,128]{1,0:T(8,128)}, u32[]{:S(2)}) copy-start(f32[512,128]{1,0:T(8,128)} %right_ref.5) | copy-start | bytes 786436
  14.0 16.1 %copy-start.1 = (f32[2,512]{1,0:T(2,128)S(1)}, f32[2,512]{1,0:T(2,128)}, u32[]{:S(2)}) copy-start(f32[2,512]{1,0:T(2,128)} %pivot_ref.3) | copy-start | bytes 12292
  26.3 3.8 %collective-permute-start = (bf16[16,2,16,512]{3,2,1,0:T(8,128)(2,1)S(1)}, bf16[16,2,16,512]{3,2,1,0:T(8,128)(2,1)S(1)}, u32[]{:S(2)}, u32[]{:S(2)}) collective-permute-start(bf16[16,2,16,512]{3,2,1,0:T(8,128)(2,1)S(1)} %bitcast.12), channel_id=1, source_target_pairs={{0,1},{1,0},{2,3},{3,2},{4,5},{5,4},{6,7},{7,6},{8,9},{9,8},{10,11... | collective-permute-start | bytes 1572872 | tf_op jit(solution)/shard_map/ppermute | solution.py:215
  30.2 8.4 %collective-permute-start.1 = (f16[128,640]{1,0:T(8,128)(2,1)S(1)}, f16[128,640]{1,0:T(8,128)(2,1)S(1)}, u32[]{:S(2)}, u32[]{:S(2)}) collective-permute-start(f16[128,640]{1,0:T(8,128)(2,1)S(1)} %convert_element_type.12), channel_id=1, source_target_pairs={{0,32},{1,33},{2,34},{3,35},{4,36},{5,37},{6,38},{7,39},{8,40},{9,... | collective-permute-start | bytes 491528 | tf_op jit(solution)/shard_map/ppermute | solution.py:221

commit v5 on v4

--- a/solution.py
+++ b/solution.py
@@ -127,8 +127,14 @@
     ]
 
 
-def first_kernel(own_ref, other_ref, pivot_ref, right_ref, x_ref, sent_ref, panel_ref):
-    me, core = lax.axis_index(ROW), lax.axis_index("c")
+def scaled_rows(x):
+    largest = jnp.max(jnp.abs(x), axis=0, keepdims=True)
+    power = jnp.clip(jnp.ceil(jnp.log2(largest)), -100.0, 127.0)
+    return jnp.concatenate([x * jnp.exp2(SPAN - power), jnp.broadcast_to(power, (8, x.shape[1]))], axis=0)
+
+
+def assemble(panel_ref, own_ref, other_ref):
+    core = lax.axis_index("c")
     groups, count, w, _ = own_ref.shape
     for k in range(count):
         into = panel_ref.at[k]
@@ -136,12 +142,21 @@
             into[pl.ds(pl.multiple_of((2 * g + core) * w, w), w)] = own_ref[g, k]
             into[pl.ds(pl.multiple_of((2 * g + 1 - core) * w, w), w)] = other_ref[g, k]
 
+
+def first_kernel(own_ref, other_ref, pivot_ref, right_ref, x_ref, sent_ref, hop_ref, panel_ref):
+    me = lax.axis_index(ROW)
+
+    @pl.when(me < panel_ref.shape[0])
+    def _():
+        assemble(panel_ref, own_ref, other_ref)
+
     @pl.when(me == 0)
     def _():
         inverse = invert_panel(panel_ref.at[0], pivot_ref[0:1])
         x = substitute(inverse, lambda n, j: panel_ref[0, :n, j * BIG : (j + 1) * BIG], right_ref[...].T)
         x_ref[...] = x
         sent_ref[...] = scaled(x)
+        hop_ref[...] = scaled_rows(x)
 
 
 def invert_kernel(panel_ref, pivot_ref, right_ref, inv_ref, turned_ref):
@@ -152,10 +167,6 @@
             inv_ref[i] = inv
 
 
-def unscaled(got):
-    return got[:, :-BLK] * jnp.exp2(got[:, -BLK : 1 - BLK] - SPAN)
-
-
 def second_kernel(got_ref, panel_ref, inv_ref, turned_ref, x_ref, sent_ref, out_ref, out_sent_ref):
     me = lax.axis_index(ROW)
 
@@ -167,24 +178,32 @@
     @pl.when(me == 1)
     def _():
         inverse = [inv_ref[i] for i in range(inv_ref.shape[0])]
-        right = turned_ref[...] - dot_exact_right(unscaled(got_ref[...]), panel_ref[0])
+        x = got_ref[:-8] * jnp.exp2(got_ref[-8:-7] - SPAN)
+        right = turned_ref[...] - dot_exact_right(x, panel_ref[0])
         x = substitute(inverse, lambda n, j: panel_ref[1, :n, j * BIG : (j + 1) * BIG], right)
         out_ref[...] = x
         out_sent_ref[...] = scaled(x)
 
 
-def last_kernel(panel_ref, pieces_ref, x_ref, right_ref, out_ref):
+def last_kernel(own_ref, other_ref, pieces_ref, x_ref, right_ref, out_ref, panel_ref):
     count, width, _ = panel_ref.shape
     columns = x_ref.shape[0]
-    got = pieces_ref[...].reshape(columns, count * width + BLK)
-    update = 0.0
-    for k in range(count):
-        at = count * width + k * BLK // count
-        x = got[:, k * width : (k + 1) * width] * jnp.exp2(got[:, at : at + 1] - SPAN)
-        update = update + dot_exact_right(x, panel_ref[k])
-    solved = lax.axis_index(ROW) < count
-    turned = jnp.where(solved, x_ref[...], update).T
-    out_ref[...] = jnp.where(solved, turned, right_ref[...] - turned)
+    me = lax.axis_index(ROW)
+
+    @pl.when(me < count)
+    def _():
+        out_ref[...] = x_ref[...].T
+
+    @pl.when(me >= count)
+    def _():
+        assemble(panel_ref, own_ref, other_ref)
+        got = pieces_ref[...].reshape(columns, count * width + BLK)
+        update = 0.0
+        for k in range(count):
+            at = count * width + k * BLK // count
+            x = got[:, k * width : (k + 1) * width] * jnp.exp2(got[:, at : at + 1] - SPAN)
+            update = update + dot_exact_right(x, panel_ref[k])
+        out_ref[...] = right_ref[...] - update.T
 
 
 def on_chip(kernel, out_shape, n_in, scratch=()):
@@ -212,13 +231,16 @@
 
     piece = jnp.swapaxes(factor, 1, 2)
     own = same_to_all(same_to_all(piece, "zl"), "x").reshape(-1, count, w, rows)
-    other = lax.ppermute(own, "c", [(0, 1), (1, 0)])
+    swap = [[(2 * r + c, 2 * r + 1 - c) for r in group for c in (0, 1)] for group in (range(count), range(count, n))]
+    other = lax.ppermute(own, ROW + ("c",), swap[0])
+    other_late = lax.ppermute(own, ROW + ("c",), swap[1])
 
     solved = (jax.ShapeDtypeStruct((columns, width), F32), jax.ShapeDtypeStruct((columns, width + BLK), F32))
     all_cols = (jax.ShapeDtypeStruct((count, width, rows), BF16),)
     kept = (jax.ShapeDtypeStruct((width // BIG, BIG, BIG), F32), jax.ShapeDtypeStruct((columns, width), F32))
-    x, sent, panel = on_chip(first_kernel, solved + all_cols, 4)(own, other, pivots, right)
-    got = lax.ppermute(sent.astype(jnp.float16), ROW, [(0, 1)])
+    hop = (jax.ShapeDtypeStruct((columns + 8, width), F32),)
+    x, sent, hop, panel = on_chip(first_kernel, solved + hop + all_cols, 4)(own, other, pivots, right)
+    got = lax.ppermute(hop.astype(jnp.float16), ROW, [(0, 1)])
     inverse, turned = on_chip(invert_kernel, kept, 3)(panel, pivots, right)
     x, sent = on_chip(second_kernel, solved, 6)(got.astype(F32), panel, inverse, turned, x, sent)
     sent = sent.astype(jnp.float16).reshape(n, columns // n, width + BLK)
@@ -227,7 +249,9 @@
     power = [mine[k, :, width + k * share : width + (k + 1) * share] for k in range(count)]
     mine = jnp.concatenate([mine[k, :, :width] for k in range(count)] + power, axis=1)
     pieces = same_to_all(mine, ROW).astype(F32)
-    return on_chip(last_kernel, jax.ShapeDtypeStruct((rows, columns), F32), 4)(panel, pieces, x, right)
+    scratch = [pltpu.VMEM((count, width, rows), BF16)]
+    out = jax.ShapeDtypeStruct((rows, columns), F32)
+    return on_chip(last_kernel, out, 5, scratch)(own, other_late, pieces, x, right)
 
 
 def solution(mesh):

time: 76.8 us -> 74.1 us (0.965)
  blocking collectives: 60.7 us -> 40.7 us
  waiting for transfers between devices: 7.33 us -> 19.8 us
  starting transfers between devices: 3.2 us -> 7.86 us
    all_to_all x3 -> x2, blocking collectives: 43.4 us -> 25.4 us  [same_to_all(): lax.all_to_all(jnp.broadcast_to(piece[None], (count, *piece.shape)), axes...]
    all_to_all x0 -> x1, waiting for transfers between devices: none -> 12.9 us  [same_to_all(): lax.all_to_all(jnp.broadcast_to(piece[None], (count, *piece.shape)), axes...]
    all_to_all x0 -> x1, starting transfers between devices: none -> 3.97 us  [same_to_all(): lax.all_to_all(jnp.broadcast_to(piece[None], (count, *piece.shape)), axes...]
    all_to_all x1, blocking collectives: 17.3 us -> 15.2 us  [whole(): mine = lax.all_to_all(sent, ROW, 0, 0, tiled=True)[:count]]
    ppermute x2 -> x3, starting transfers between devices: 3.2 us -> 3.88 us  [the longest x1 1.91 us: whole(): other = lax.ppermute(own, ROW + ('c',), swap[0])]
    ppermute x2 -> x3, waiting for transfers between devices: 7.33 us -> 6.82 us  [the longest x1 4.94 us: whole(): got = lax.ppermute(hop.astype(jnp.float16), ROW, [(0, 1)])]
  transfers between devices with their start and end apart: 2 -> 4, of which waited for: 2 -> 3; matrix products, arithmetic and copies ran while one was open for 0% -> 0% of each run, Pallas kernels for 2% -> 2%
where the time goes in v5:
time: 74.1 us; the launch traced here: 73.7 us
  blocking collectives  40.7 us (55%)
  waiting for transfers between devices  19.8 us (27%)
  starting transfers between devices  7.86 us (11%)
  Pallas kernels  3.44 us (5%)
  local copies, waits for them, and re-layouts  1.73 us (2%)
    all_to_all x2, blocking collectives, same_to_all(): lax.all_to_all(jnp.broadcast_to(piece[None], (count, *piece.shape)), axes...  25.4 us
    all_to_all x1, blocking collectives, whole(): mine = lax.all_to_all(sent, ROW, 0, 0, tiled=True)[:count]  15.2 us
    all_to_all x1, waiting for transfers between devices, same_to_all(): lax.all_to_all(jnp.broadcast_to(piece[None], (count, *piece.shape)), axes...  12.9 us
    ppermute x1, waiting for transfers between devices, whole(): got = lax.ppermute(hop.astype(jnp.float16), ROW, [(0, 1)])  4.94 us
    all_to_all x1, starting transfers between devices, same_to_all(): lax.all_to_all(jnp.broadcast_to(piece[None], (count, *piece.shape)), axes...  3.97 us
    ppermute x1, starting transfers between devices, whole(): other = lax.ppermute(own, ROW + ('c',), swap[0])  1.91 us
    ppermute x1, waiting for transfers between devices, whole(): other = lax.ppermute(own, ROW + ('c',), swap[0])  1.88 us
    pallas_call x1, Pallas kernels, whole(): inverse, turned = on_chip(invert_kernel, kept, 3)(panel, pivots, right)  1.58 us
  transfers between devices with their start and end apart: 4, of which 3 were waited for; matrix products, arithmetic and copies ran while one was open for 0% of the time, Pallas kernels for 2%

profile of v5, /device:TPU:8, one launch (start us, length us, event | category | flops | bytes accessed | tf_op | source)
XLA Modules:
  0.0 73.7 jit_solution(11697828269011417198)
XLA Ops:
  0.0 0.8 %broadcast_in_dim.6 = bf16[4,2,16,512]{3,2,1,0:T(8,128)(2,1)S(1)} broadcast(bf16[2,16,512]{2,1,0:T(8,128)(2,1)} %bitcast.16), dimensions={1,2,3} | broadcast | bytes 163840 | tf_op jit(solution)/shard_map/broadcast_in_dim | solution.py:223
  0.8 13.1 %all_to_all.20 = bf16[4,2,16,512]{3,2,1,0:T(8,128)(2,1)S(1)} all-to-all(bf16[4,2,16,512]{3,2,1,0:T(8,128)(2,1)S(1)} %broadcast_in_dim.6), channel_id=1, replica_groups=mesh['zh'=2,'yh'=4,'yl'=2,'x'=4,'zl'=4,'c'=2] {'zl'}, dimensions={0} | all-to-all | bytes 262144 | tf_op jit(solution)/shard_map/all_to_all | solution.py:223
  14.0 0.0 copy-start
  14.0 0.0 copy-start.1
  14.0 12.3 %all_to_all.21 = bf16[4,4,2,16,512]{4,3,2,1,0:T(8,128)(2,1)S(1)} all-to-all(bf16[4,4,2,16,512]{4,3,2,1,0:T(8,128)(2,1)S(1)} %broadcast_in_dim.7), channel_id=1, replica_groups=mesh['zh'=2,'yh'=4,'yl'=2,'x'=4,'zl'=4,'c'=2] {'x'}, dimensions={0} | all-to-all | bytes 1048576 | tf_op jit(solution)/shard_map/all_to_all | solution.py:223
  26.3 1.9 %collective-permute-start.1 = (bf16[16,2,16,512]{3,2,1,0:T(8,128)(2,1)S(1)}, bf16[16,2,16,512]{3,2,1,0:T(8,128)(2,1)S(1)}, u32[]{:S(2)}, u32[]{:S(2)}) collective-permute-start(bf16[16,2,16,512]{3,2,1,0:T(8,128)(2,1)S(1)} %bitcast.12), channel_id=1, source_target_pairs={{0,1},{1,0},{32,33},{33,32},{2,3},{3,2},{34,35},{35,34},{4,5},{5,4... | collective-permute-start | bytes 1572872 | tf_op jit(solution)/shard_map/ppermute | solution.py:235
  28.2 1.9 %collective-permute-done.1.other_ref = bf16[16,2,16,512]{3,2,1,0:T(8,128)(2,1)S(1)} collective-permute-done((bf16[16,2,16,512]{3,2,1,0:T(8,128)(2,1)S(1)}, bf16[16,2,16,512]{3,2,1,0:T(8,128)(2,1)S(1)}, u32[]{:S(2)}, u32[]{:S(2)}) %collective-permute-start.1) | collective-permute-done | bytes 524320 | tf_op jit(solution)/shard_map/ppermute | solution.py:235
  30.1 0.0 copy-done
  30.1 0.0 copy-done.1
  30.1 0.1 shard_map.37
  30.2 1.3 %collective-permute-start.2 = (f16[136,512]{1,0:T(8,128)(2,1)S(1)}, f16[136,512]{1,0:T(8,128)(2,1)S(1)}, u32[]{:S(2)}, u32[]{:S(2)}) collective-permute-start(f16[136,512]{1,0:T(8,128)(2,1)S(1)} %convert_element_type.12), channel_id=1, source_target_pairs={{0,32},{1,33},{2,34},{3,35},{4,36},{5,37},{6,38},{7,39},{8,40},{9,... | collective-permute-start | bytes 417800 | tf_op jit(solution)/shard_map/ppermute | solution.py:243
  31.5 1.6 %shard_map.38 = (f32[2,256,256]{2,1,0:T(8,128)S(1)}, f32[128,512]{1,0:T(8,128)S(1)}) custom-call(bf16[2,512,512]{2,1,0:T(8,128)(2,1)S(1)} %get-tuple-element.14.panel_ref, f32[2,512]{1,0:T(2,128)S(1)} %copy-done.1, f32[512,128]{1,0:T(8,128)S(1)} %copy-done), custom_call_target="tpu_custom_call" | custom-call | tf_op jit(solution)/shard_map/pallas_call | solution.py:244
  33.1 4.9 %collective-permute-done.2 = f16[136,512]{1,0:T(8,128)(2,1)S(1)} collective-permute-done((f16[136,512]{1,0:T(8,128)(2,1)S(1)}, f16[136,512]{1,0:T(8,128)(2,1)S(1)}, u32[]{:S(2)}, u32[]{:S(2)}) %collective-permute-start.2) | collective-permute-done | bytes 139296 | tf_op jit(solution)/shard_map/ppermute | solution.py:243
  38.1 0.9 %shard_map.39 = (f32[128,512]{1,0:T(8,128)S(1)}, f32[128,640]{1,0:T(8,128)S(1)}) custom-call(f32[136,512]{1,0:T(8,128)S(1)} %convert_element_type.13.got_ref, bf16[2,512,512]{2,1,0:T(8,128)(2,1)S(1)} %get-tuple-element.14.panel_ref, f32[2,256,256]{2,1,0:T(8,128)S(1)} %get-tuple-element.15.inv_ref, f32[128,512]{1,0:T(8,128)S(1)} %get-tuple-element.16.turned_ref, ...), custom_call_target="tpu_custom_call" | custom-call | tf_op jit(solution)/shard_map/pallas_call | solution.py:245
  39.0 15.2 %all_to_all.22 = f16[16,8,640]{2,1,0:T(8,128)(2,1)S(1)} all-to-all(f16[16,8,640]{2,1,0:T(8,128)(2,1)S(1)} %convert_bitcast_fusion), channel_id=1, replica_groups=mesh['zh'=2,'yh'=4,'yl'=2,'x'=4,'zl'=4,'c'=2] {'zh','yh','yl'}, dimensions={0} | all-to-all | bytes 327680 | tf_op jit(solution)/shard_map/all_to_all | solution.py:247
  54.3 0.1 slice_bitcast_fusion.2
  54.3 0.1 concatenate.3
  54.4 0.7 broadcast_in_dim.8
  55.2 4.0 %all-to-all-start.3 = ((f16[16,8,1152]{2,1,0:T(8,128)(2,1)}), f16[16,8,1152]{2,1,0:T(8,128)(2,1)S(1)}, u32[]{:S(2)}, u32[]{:S(2)}) async-start(f16[16,8,1152]{2,1,0:T(8,128)(2,1)} %broadcast_in_dim.8), calls=%async_computation.3 | async-start | bytes 589824 | tf_op jit(solution)/shard_map/all_to_all | solution.py:223
  59.1 0.7 collective-permute-start
  59.8 12.9 %all-to-all-done.3 = f16[16,8,1152]{2,1,0:T(8,128)(2,1)S(1)} async-done(((f16[16,8,1152]{2,1,0:T(8,128)(2,1)}), f16[16,8,1152]{2,1,0:T(8,128)(2,1)S(1)}, u32[]{:S(2)}, u32[]{:S(2)}) %all-to-all-start.3) | async-done | bytes 294944 | tf_op jit(solution)/shard_map/all_to_all | solution.py:223
  72.8 0.0 collective-permute-done.other_ref
  72.8 0.9 %shard_map.40 = f32[512,128]{1,0:T(8,128)} custom-call(bf16[16,2,16,512]{3,2,1,0:T(8,128)(2,1)S(1)} %bitcast.15, bf16[16,2,16,512]{3,2,1,0:T(8,128)(2,1)S(1)} %collective-permute-done.other_ref, f32[16,8,1152]{2,1,0:T(8,128)S(1)} %convert_element_type.15.pieces_ref, f32[128,512]{1,0:T(8,128)S(1)} %get-tuple-element.20.x_ref, f32[512,128]{1,0:T(8,128)S(1)} %copy-done), custom_call_target="tpu_custom_call" | custom-call | tf_op jit(solution)/shard_map/pallas_call | solution.py:254
  (6 shorter events, 0.2 us)
Async XLA Ops:
  14.0 16.1 %copy-start = (f32[512,128]{1,0:T(8,128)S(1)}, f32[512,128]{1,0:T(8,128)}, u32[]{:S(2)}) copy-start(f32[512,128]{1,0:T(8,128)} %right_ref.5) | copy-start | bytes 786436
  14.0 16.1 %copy-start.1 = (f32[2,512]{1,0:T(2,128)S(1)}, f32[2,512]{1,0:T(2,128)}, u32[]{:S(2)}) copy-start(f32[2,512]{1,0:T(2,128)} %pivot_ref.3) | copy-start | bytes 12292
  26.3 3.8 %collective-permute-start.1 = (bf16[16,2,16,512]{3,2,1,0:T(8,128)(2,1)S(1)}, bf16[16,2,16,512]{3,2,1,0:T(8,128)(2,1)S(1)}, u32[]{:S(2)}, u32[]{:S(2)}) collective-permute-start(bf16[16,2,16,512]{3,2,1,0:T(8,128)(2,1)S(1)} %bitcast.12), channel_id=1, source_target_pairs={{0,1},{1,0},{32,33},{33,32},{2,3},{3,2},{34,35},{35,34},{4,5},{5,4... | collective-permute-start | bytes 1572872 | tf_op jit(solution)/shard_map/ppermute | solution.py:235
  30.2 7.8 %collective-permute-start.2 = (f16[136,512]{1,0:T(8,128)(2,1)S(1)}, f16[136,512]{1,0:T(8,128)(2,1)S(1)}, u32[]{:S(2)}, u32[]{:S(2)}) collective-permute-start(f16[136,512]{1,0:T(8,128)(2,1)S(1)} %convert_element_type.12), channel_id=1, source_target_pairs={{0,32},{1,33},{2,34},{3,35},{4,36},{5,37},{6,38},{7,39},{8,40},{9,... | collective-permute-start | bytes 417800 | tf_op jit(solution)/shard_map/ppermute | solution.py:243
  55.2 17.6 %all-to-all-start.3 = ((f16[16,8,1152]{2,1,0:T(8,128)(2,1)}), f16[16,8,1152]{2,1,0:T(8,128)(2,1)S(1)}, u32[]{:S(2)}, u32[]{:S(2)}) async-start(f16[16,8,1152]{2,1,0:T(8,128)(2,1)} %broadcast_in_dim.8), calls=%async_computation.3 | async-start | bytes 589824 | tf_op jit(solution)/shard_map/all_to_all | solution.py:223
  59.1 13.7 %collective-permute-start = (bf16[16,2,16,512]{3,2,1,0:T(8,128)(2,1)S(1)}, bf16[16,2,16,512]{3,2,1,0:T(8,128)(2,1)S(1)}, u32[]{:S(2)}, u32[]{:S(2)}) collective-permute-start(bf16[16,2,16,512]{3,2,1,0:T(8,128)(2,1)S(1)} %bitcast.14), channel_id=1, source_target_pairs={{64,65},{65,64},{96,97},{97,96},{128,129},{129,128},{160,161},{161... | collective-permute-start | bytes 1572872 | tf_op jit(solution)/shard_map/ppermute | solution.py:236

commit v6 on v5

--- a/solution.py
+++ b/solution.py
@@ -111,10 +111,20 @@
     return jnp.concatenate(xs, axis=1)
 
 
+def power_of(largest):
+    return jnp.clip(jnp.ceil(jnp.log2(largest)), -100.0, 127.0)
+
+
 def scaled(x):
-    largest = jnp.max(jnp.abs(x), axis=1, keepdims=True)
-    power = jnp.clip(jnp.ceil(jnp.log2(largest)), -100.0, 127.0)
-    return jnp.concatenate([x * jnp.exp2(SPAN - power), jnp.broadcast_to(power, (x.shape[0], BLK))], axis=1)
+    blocks = x.shape[1] // BLK
+    lane = iota((x.shape[0], BLK), 1) // (BLK // 2 // blocks) % blocks
+    out, powers = [], jnp.zeros((x.shape[0], BLK), F32)
+    for j in range(blocks):
+        part = x[:, j * BLK : (j + 1) * BLK]
+        power = power_of(jnp.max(jnp.abs(part), axis=1, keepdims=True))
+        out.append(part * jnp.exp2(SPAN - power))
+        powers = jnp.where(lane == j, power, powers)
+    return jnp.concatenate(out + [powers], axis=1)
 
 
 def invert_panel(panel, pivot):
@@ -128,8 +138,7 @@
 
 
 def scaled_rows(x):
-    largest = jnp.max(jnp.abs(x), axis=0, keepdims=True)
-    power = jnp.clip(jnp.ceil(jnp.log2(largest)), -100.0, 127.0)
+    power = power_of(jnp.max(jnp.abs(x), axis=0, keepdims=True))
     return jnp.concatenate([x * jnp.exp2(SPAN - power), jnp.broadcast_to(power, (8, x.shape[1]))], axis=0)
 
 
@@ -200,9 +209,13 @@
         got = pieces_ref[...].reshape(columns, count * width + BLK)
         update = 0.0
         for k in range(count):
-            at = count * width + k * BLK // count
-            x = got[:, k * width : (k + 1) * width] * jnp.exp2(got[:, at : at + 1] - SPAN)
-            update = update + dot_exact_right(x, panel_ref[k])
+            parts = []
+            for j in range(width // BLK):
+                at = k * width + j * BLK
+                lane = count * width + at * BLK // (count * width)
+                power = got[:, lane : lane + 1]
+                parts.append(got[:, at : at + BLK] * jnp.exp2(power - SPAN))
+            update = update + dot_exact_right(jnp.concatenate(parts, axis=1), panel_ref[k])
         out_ref[...] = right_ref[...] - update.T
 
 

time: 74.1 us -> 74.1 us (level)
  no operation moved by 1% of the time
where the time goes in v6:
time: 74.1 us; the launch traced here: 73.7 us
  blocking collectives  40.7 us (55%)
  waiting for transfers between devices  19.8 us (27%)
  starting transfers between devices  7.86 us (11%)
  Pallas kernels  3.44 us (5%)
  local copies, waits for them, and re-layouts  1.73 us (2%)
    all_to_all x2, blocking collectives, same_to_all(): lax.all_to_all(jnp.broadcast_to(piece[None], (count, *piece.shape)), axes...  25.4 us
    all_to_all x1, blocking collectives, whole(): mine = lax.all_to_all(sent, ROW, 0, 0, tiled=True)[:count]  15.2 us
    all_to_all x1, waiting for transfers between devices, same_to_all(): lax.all_to_all(jnp.broadcast_to(piece[None], (count, *piece.shape)), axes...  13 us
    ppermute x1, waiting for transfers between devices, whole(): got = lax.ppermute(hop.astype(jnp.float16), ROW, [(0, 1)])  4.95 us
    all_to_all x1, starting transfers between devices, same_to_all(): lax.all_to_all(jnp.broadcast_to(piece[None], (count, *piece.shape)), axes...  3.97 us
    ppermute x1, starting transfers between devices, whole(): other = lax.ppermute(own, ROW + ('c',), swap[0])  1.91 us
    ppermute x1, waiting for transfers between devices, whole(): other = lax.ppermute(own, ROW + ('c',), swap[0])  1.88 us
    pallas_call x1, Pallas kernels, whole(): inverse, turned = on_chip(invert_kernel, kept, 3)(panel, pivots, right)  1.58 us
  transfers between devices with their start and end apart: 4, of which 3 were waited for; matrix products, arithmetic and copies ran while one was open for 0% of the time, Pallas kernels for 2%

profile of v6, /device:TPU:8, one launch (start us, length us, event | category | flops | bytes accessed | tf_op | source)
XLA Modules:
  0.0 73.7 jit_solution(13362959021955582132)
XLA Ops:
  0.0 0.8 %broadcast_in_dim.6 = bf16[4,2,16,512]{3,2,1,0:T(8,128)(2,1)S(1)} broadcast(bf16[2,16,512]{2,1,0:T(8,128)(2,1)} %bitcast.16), dimensions={1,2,3} | broadcast | bytes 163840 | tf_op jit(solution)/shard_map/broadcast_in_dim | solution.py:236
  0.8 13.1 %all_to_all.20 = bf16[4,2,16,512]{3,2,1,0:T(8,128)(2,1)S(1)} all-to-all(bf16[4,2,16,512]{3,2,1,0:T(8,128)(2,1)S(1)} %broadcast_in_dim.6), channel_id=1, replica_groups=mesh['zh'=2,'yh'=4,'yl'=2,'x'=4,'zl'=4,'c'=2] {'zl'}, dimensions={0} | all-to-all | bytes 262144 | tf_op jit(solution)/shard_map/all_to_all | solution.py:236
  14.0 0.0 copy-start
  14.0 0.0 copy-start.1
  14.0 12.3 %all_to_all.21 = bf16[4,4,2,16,512]{4,3,2,1,0:T(8,128)(2,1)S(1)} all-to-all(bf16[4,4,2,16,512]{4,3,2,1,0:T(8,128)(2,1)S(1)} %broadcast_in_dim.7), channel_id=1, replica_groups=mesh['zh'=2,'yh'=4,'yl'=2,'x'=4,'zl'=4,'c'=2] {'x'}, dimensions={0} | all-to-all | bytes 1048576 | tf_op jit(solution)/shard_map/all_to_all | solution.py:236
  26.3 1.9 %collective-permute-start.1 = (bf16[16,2,16,512]{3,2,1,0:T(8,128)(2,1)S(1)}, bf16[16,2,16,512]{3,2,1,0:T(8,128)(2,1)S(1)}, u32[]{:S(2)}, u32[]{:S(2)}) collective-permute-start(bf16[16,2,16,512]{3,2,1,0:T(8,128)(2,1)S(1)} %bitcast.12), channel_id=1, source_target_pairs={{0,1},{1,0},{32,33},{33,32},{2,3},{3,2},{34,35},{35,34},{4,5},{5,4... | collective-permute-start | bytes 1572872 | tf_op jit(solution)/shard_map/ppermute | solution.py:248
  28.2 1.9 %collective-permute-done.1.other_ref = bf16[16,2,16,512]{3,2,1,0:T(8,128)(2,1)S(1)} collective-permute-done((bf16[16,2,16,512]{3,2,1,0:T(8,128)(2,1)S(1)}, bf16[16,2,16,512]{3,2,1,0:T(8,128)(2,1)S(1)}, u32[]{:S(2)}, u32[]{:S(2)}) %collective-permute-start.1) | collective-permute-done | bytes 524320 | tf_op jit(solution)/shard_map/ppermute | solution.py:248
  30.1 0.0 copy-done
  30.1 0.0 copy-done.1
  30.1 0.1 shard_map.37
  30.2 1.3 %collective-permute-start.2 = (f16[136,512]{1,0:T(8,128)(2,1)S(1)}, f16[136,512]{1,0:T(8,128)(2,1)S(1)}, u32[]{:S(2)}, u32[]{:S(2)}) collective-permute-start(f16[136,512]{1,0:T(8,128)(2,1)S(1)} %convert_element_type.12), channel_id=1, source_target_pairs={{0,32},{1,33},{2,34},{3,35},{4,36},{5,37},{6,38},{7,39},{8,40},{9,... | collective-permute-start | bytes 417800 | tf_op jit(solution)/shard_map/ppermute | solution.py:256
  31.5 1.6 %shard_map.38 = (f32[2,256,256]{2,1,0:T(8,128)S(1)}, f32[128,512]{1,0:T(8,128)S(1)}) custom-call(bf16[2,512,512]{2,1,0:T(8,128)(2,1)S(1)} %get-tuple-element.14.panel_ref, f32[2,512]{1,0:T(2,128)S(1)} %copy-done.1, f32[512,128]{1,0:T(8,128)S(1)} %copy-done), custom_call_target="tpu_custom_call" | custom-call | tf_op jit(solution)/shard_map/pallas_call | solution.py:257
  33.1 4.9 %collective-permute-done.2 = f16[136,512]{1,0:T(8,128)(2,1)S(1)} collective-permute-done((f16[136,512]{1,0:T(8,128)(2,1)S(1)}, f16[136,512]{1,0:T(8,128)(2,1)S(1)}, u32[]{:S(2)}, u32[]{:S(2)}) %collective-permute-start.2) | collective-permute-done | bytes 139296 | tf_op jit(solution)/shard_map/ppermute | solution.py:256
  38.1 0.9 %shard_map.39 = (f32[128,512]{1,0:T(8,128)S(1)}, f32[128,640]{1,0:T(8,128)S(1)}) custom-call(f32[136,512]{1,0:T(8,128)S(1)} %convert_element_type.13.got_ref, bf16[2,512,512]{2,1,0:T(8,128)(2,1)S(1)} %get-tuple-element.14.panel_ref, f32[2,256,256]{2,1,0:T(8,128)S(1)} %get-tuple-element.15.inv_ref, f32[128,512]{1,0:T(8,128)S(1)} %get-tuple-element.16.turned_ref, ...), custom_call_target="tpu_custom_call" | custom-call | tf_op jit(solution)/shard_map/pallas_call | solution.py:258
  39.0 15.2 %all_to_all.22 = f16[16,8,640]{2,1,0:T(8,128)(2,1)S(1)} all-to-all(f16[16,8,640]{2,1,0:T(8,128)(2,1)S(1)} %convert_bitcast_fusion), channel_id=1, replica_groups=mesh['zh'=2,'yh'=4,'yl'=2,'x'=4,'zl'=4,'c'=2] {'zh','yh','yl'}, dimensions={0} | all-to-all | bytes 327680 | tf_op jit(solution)/shard_map/all_to_all | solution.py:260
  54.3 0.1 slice_bitcast_fusion.2
  54.4 0.1 concatenate.3
  54.5 0.7 broadcast_in_dim.8
  55.2 4.0 %all-to-all-start.3 = ((f16[16,8,1152]{2,1,0:T(8,128)(2,1)}), f16[16,8,1152]{2,1,0:T(8,128)(2,1)S(1)}, u32[]{:S(2)}, u32[]{:S(2)}) async-start(f16[16,8,1152]{2,1,0:T(8,128)(2,1)} %broadcast_in_dim.8), calls=%async_computation.3 | async-start | bytes 589824 | tf_op jit(solution)/shard_map/all_to_all | solution.py:236
  59.2 0.7 collective-permute-start
  59.8 13.0 %all-to-all-done.3 = f16[16,8,1152]{2,1,0:T(8,128)(2,1)S(1)} async-done(((f16[16,8,1152]{2,1,0:T(8,128)(2,1)}), f16[16,8,1152]{2,1,0:T(8,128)(2,1)S(1)}, u32[]{:S(2)}, u32[]{:S(2)}) %all-to-all-start.3) | async-done | bytes 294944 | tf_op jit(solution)/shard_map/all_to_all | solution.py:236
  72.8 0.0 collective-permute-done.other_ref
  72.9 0.9 %shard_map.40 = f32[512,128]{1,0:T(8,128)} custom-call(bf16[16,2,16,512]{3,2,1,0:T(8,128)(2,1)S(1)} %bitcast.15, bf16[16,2,16,512]{3,2,1,0:T(8,128)(2,1)S(1)} %collective-permute-done.other_ref, f32[16,8,1152]{2,1,0:T(8,128)S(1)} %convert_element_type.15.pieces_ref, f32[128,512]{1,0:T(8,128)S(1)} %get-tuple-element.20.x_ref, f32[512,128]{1,0:T(8,128)S(1)} %copy-done), custom_call_target="tpu_custom_call" | custom-call | tf_op jit(solution)/shard_map/pallas_call | solution.py:267
  (6 shorter events, 0.2 us)
Async XLA Ops:
  14.0 16.1 %copy-start = (f32[512,128]{1,0:T(8,128)S(1)}, f32[512,128]{1,0:T(8,128)}, u32[]{:S(2)}) copy-start(f32[512,128]{1,0:T(8,128)} %right_ref.5) | copy-start | bytes 786436
  14.0 16.1 %copy-start.1 = (f32[2,512]{1,0:T(2,128)S(1)}, f32[2,512]{1,0:T(2,128)}, u32[]{:S(2)}) copy-start(f32[2,512]{1,0:T(2,128)} %pivot_ref.3) | copy-start | bytes 12292
  26.3 3.8 %collective-permute-start.1 = (bf16[16,2,16,512]{3,2,1,0:T(8,128)(2,1)S(1)}, bf16[16,2,16,512]{3,2,1,0:T(8,128)(2,1)S(1)}, u32[]{:S(2)}, u32[]{:S(2)}) collective-permute-start(bf16[16,2,16,512]{3,2,1,0:T(8,128)(2,1)S(1)} %bitcast.12), channel_id=1, source_target_pairs={{0,1},{1,0},{32,33},{33,32},{2,3},{3,2},{34,35},{35,34},{4,5},{5,4... | collective-permute-start | bytes 1572872 | tf_op jit(solution)/shard_map/ppermute | solution.py:248
  30.2 7.8 %collective-permute-start.2 = (f16[136,512]{1,0:T(8,128)(2,1)S(1)}, f16[136,512]{1,0:T(8,128)(2,1)S(1)}, u32[]{:S(2)}, u32[]{:S(2)}) collective-permute-start(f16[136,512]{1,0:T(8,128)(2,1)S(1)} %convert_element_type.12), channel_id=1, source_target_pairs={{0,32},{1,33},{2,34},{3,35},{4,36},{5,37},{6,38},{7,39},{8,40},{9,... | collective-permute-start | bytes 417800 | tf_op jit(solution)/shard_map/ppermute | solution.py:256
  55.2 17.6 %all-to-all-start.3 = ((f16[16,8,1152]{2,1,0:T(8,128)(2,1)}), f16[16,8,1152]{2,1,0:T(8,128)(2,1)S(1)}, u32[]{:S(2)}, u32[]{:S(2)}) async-start(f16[16,8,1152]{2,1,0:T(8,128)(2,1)} %broadcast_in_dim.8), calls=%async_computation.3 | async-start | bytes 589824 | tf_op jit(solution)/shard_map/all_to_all | solution.py:236
  59.2 13.7 %collective-permute-start = (bf16[16,2,16,512]{3,2,1,0:T(8,128)(2,1)S(1)}, bf16[16,2,16,512]{3,2,1,0:T(8,128)(2,1)S(1)}, u32[]{:S(2)}, u32[]{:S(2)}) collective-permute-start(bf16[16,2,16,512]{3,2,1,0:T(8,128)(2,1)S(1)} %bitcast.14), channel_id=1, source_target_pairs={{64,65},{65,64},{96,97},{97,96},{128,129},{129,128},{160,161},{161... | collective-permute-start | bytes 1572872 | tf_op jit(solution)/shard_map/ppermute | solution.py:249

commit v7 on v6

--- a/solution.py
+++ b/solution.py
@@ -76,7 +76,10 @@
     one = jnp.where(row[:BASE] == lane[:BASE] % BASE, 1.0, 0.0).astype(F32)
     r = [one] * count
     for i in range(BASE - 1):
-        spread = mm(packed, jnp.where(pick == i, 1.0, 0.0).astype(BF16))
+        if i % 2 == 0:
+            two = jnp.concatenate([jnp.where(pick == i + j, 1.0, 0.0) for j in range(2)], axis=1).astype(BF16)
+            two = mm(packed, two)
+        spread = two[:, i % 2 * BLK : (i % 2 + 1) * BLK]
         top = (i + 1) // 8 * 8
         for k in range(count):
             x = r[k][i : i + 1] * recip[k][i : i + 1]
@@ -152,17 +155,17 @@
             into[pl.ds(pl.multiple_of((2 * g + 1 - core) * w, w), w)] = other_ref[g, k]
 
 
-def first_kernel(own_ref, other_ref, pivot_ref, right_ref, x_ref, sent_ref, hop_ref, panel_ref):
-    me = lax.axis_index(ROW)
-
-    @pl.when(me < panel_ref.shape[0])
-    def _():
-        assemble(panel_ref, own_ref, other_ref)
-
-    @pl.when(me == 0)
-    def _():
-        inverse = invert_panel(panel_ref.at[0], pivot_ref[0:1])
-        x = substitute(inverse, lambda n, j: panel_ref[0, :n, j * BIG : (j + 1) * BIG], right_ref[...].T)
+def first_kernel(cols_ref, pivot_ref, right_ref, x_ref, sent_ref, hop_ref, panel_ref):
+    cores, groups, w, _ = cols_ref.shape
+    for g in range(groups):
+        for c in range(cores):
+            at = (cores * g + c) * w
+            panel_ref[at : at + w] = cols_ref[c, g]
+
+    @pl.when(lax.axis_index(ROW) == 0)
+    def _():
+        inverse = invert_panel(panel_ref, pivot_ref[0:1])
+        x = substitute(inverse, lambda n, j: panel_ref[:n, j * BIG : (j + 1) * BIG], right_ref[...].T)
         x_ref[...] = x
         sent_ref[...] = scaled(x)
         hop_ref[...] = scaled_rows(x)
@@ -172,11 +175,13 @@
     @pl.when(lax.axis_index(ROW) == 1)
     def _():
         turned_ref[...] = right_ref[...].T
-        for i, inv in enumerate(invert_panel(panel_ref.at[1], pivot_ref[1:2])):
+        for i, inv in enumerate(invert_panel(panel_ref, pivot_ref[1:2])):
             inv_ref[i] = inv
 
 
-def second_kernel(got_ref, panel_ref, inv_ref, turned_ref, x_ref, sent_ref, out_ref, out_sent_ref):
+def second_kernel(
+    got_ref, own_ref, other_ref, panel_ref, inv_ref, turned_ref, x_ref, sent_ref, out_ref, out_sent_ref, low_ref
+):
     me = lax.axis_index(ROW)
 
     @pl.when(me == 0)
@@ -188,8 +193,9 @@
     def _():
         inverse = [inv_ref[i] for i in range(inv_ref.shape[0])]
         x = got_ref[:-8] * jnp.exp2(got_ref[-8:-7] - SPAN)
-        right = turned_ref[...] - dot_exact_right(x, panel_ref[0])
-        x = substitute(inverse, lambda n, j: panel_ref[1, :n, j * BIG : (j + 1) * BIG], right)
+        assemble(low_ref, own_ref, other_ref)
+        right = turned_ref[...] - dot_exact_right(x, low_ref[0])
+        x = substitute(inverse, lambda n, j: panel_ref[:n, j * BIG : (j + 1) * BIG], right)
         out_ref[...] = x
         out_sent_ref[...] = scaled(x)
 
@@ -243,19 +249,33 @@
     n = lax.axis_size(ROW)
 
     piece = jnp.swapaxes(factor, 1, 2)
-    own = same_to_all(same_to_all(piece, "zl"), "x").reshape(-1, count, w, rows)
-    swap = [[(2 * r + c, 2 * r + 1 - c) for r in group for c in (0, 1)] for group in (range(count), range(count, n))]
-    other = lax.ppermute(own, ROW + ("c",), swap[0])
-    other_late = lax.ppermute(own, ROW + ("c",), swap[1])
-
+    near = same_to_all(piece, "zl")
+    own = same_to_all(near, "x").reshape(-1, count, w, rows)
+    swap = [(2 * r + c, 2 * r + 1 - c) for r in range(count, n) for c in (0, 1)]
+    other_late = lax.ppermute(own, ROW + ("c",), swap)
     solved = (jax.ShapeDtypeStruct((columns, width), F32), jax.ShapeDtypeStruct((columns, width + BLK), F32))
-    all_cols = (jax.ShapeDtypeStruct((count, width, rows), BF16),)
-    kept = (jax.ShapeDtypeStruct((width // BIG, BIG, BIG), F32), jax.ShapeDtypeStruct((columns, width), F32))
-    hop = (jax.ShapeDtypeStruct((columns + 8, width), F32),)
-    x, sent, hop, panel = on_chip(first_kernel, solved + hop + all_cols, 4)(own, other, pivots, right)
-    got = lax.ppermute(hop.astype(jnp.float16), ROW, [(0, 1)])
-    inverse, turned = on_chip(invert_kernel, kept, 3)(panel, pivots, right)
-    x, sent = on_chip(second_kernel, solved, 6)(got.astype(F32), panel, inverse, turned, x, sent)
+
+    def solve(own, pivots, right):
+        me = lax.axis_index(ROW)
+        mine = lax.dynamic_index_in_dim(own, me, 1, False)
+        rest = lax.dynamic_slice_in_dim(own, 1 - me, 1, 1)
+        both = lax.all_gather(mine, "c")
+        other = jax.ShapeDtypeStruct((columns + 8, width), F32), jax.ShapeDtypeStruct((width, rows), BF16)
+        kept = (jax.ShapeDtypeStruct((width // BIG, BIG, BIG), F32), jax.ShapeDtypeStruct((columns, width), F32))
+        x, sent, hop, panel = on_chip(first_kernel, solved + other, 3)(both, pivots, right)
+        got = lax.ppermute(hop.astype(jnp.float16), ROW, [(0, 1)])
+        swap = [(2 * r + c, 2 * r + 1 - c) for r in range(count) for c in (0, 1)]
+        low = lax.ppermute(rest, ROW + ("c",), swap)
+        inverse, turned = on_chip(invert_kernel, kept, 3)(panel, pivots, right)
+        scratch = [pltpu.VMEM((1, width, rows), BF16)]
+        return on_chip(second_kernel, solved, 8, scratch)(
+            got.astype(F32), rest, low, panel, inverse, turned, x, sent
+        )
+
+    def skip(own, pivots, right):
+        return on_chip(lambda *refs: None, solved, 1)(right)
+
+    x, sent = lax.cond(lax.axis_index(ROW) < count, solve, skip, own, pivots, right)
     sent = sent.astype(jnp.float16).reshape(n, columns // n, width + BLK)
     mine = lax.all_to_all(sent, ROW, 0, 0, tiled=True)[:count]
     share = BLK // count

time: 74.1 us -> 76.4 us (1.031)
  the two profiles are of different devices: /device:TPU:8 before, /device:TPU:16 now
where the time goes in v7:
time: 76.4 us; the launch traced here: 76 us
  blocking collectives  41 us (54%)
  waiting for transfers between devices  19.6 us (26%)
  starting transfers between devices  11.4 us (15%)
  local copies, waits for them, and re-layouts  2.54 us (3%)
  Pallas kernels  1.42 us (2%)
    all_to_all x1, blocking collectives, whole(): mine = lax.all_to_all(sent, ROW, 0, 0, tiled=True)[:count]  27.8 us
    all_to_all x2, waiting for transfers between devices, same_to_all(): lax.all_to_all(jnp.broadcast_to(piece[None], (count, *piece.shape)), axes...  19.6 us
    all_to_all x1, blocking collectives, same_to_all(): lax.all_to_all(jnp.broadcast_to(piece[None], (count, *piece.shape)), axes...  13.1 us
    all_to_all x2, starting transfers between devices, same_to_all(): lax.all_to_all(jnp.broadcast_to(piece[None], (count, *piece.shape)), axes...  9.45 us
    broadcast_in_dim x3, local copies, waits for them, and re-layouts, same_to_all(): jnp.broadcast_to(piece[None], (count, *piece.shape))  2.36 us
    ppermute x1, starting transfers between devices, whole(): other_late = lax.ppermute(own, ROW + ('c',), swap)  1.91 us
  transfers between devices with their start and end apart: 3, of which 2 were waited for; matrix products, arithmetic and copies ran while one was open for 0% of the time, Pallas kernels for 0%

profile of v7, /device:TPU:16, one launch (start us, length us, event | category | flops | bytes accessed | tf_op | source)
XLA Modules:
  0.0 76.0 jit_solution(3605402539855719411)
XLA Ops:
  0.0 0.8 %broadcast_in_dim.6 = bf16[4,2,16,512]{3,2,1,0:T(8,128)(2,1)S(1)} broadcast(bf16[2,16,512]{2,1,0:T(8,128)(2,1)} %bitcast.17), dimensions={1,2,3} | broadcast | bytes 163840 | tf_op jit(solution)/shard_map/broadcast_in_dim | solution.py:242
  0.8 13.1 %all_to_all.20 = bf16[4,2,16,512]{3,2,1,0:T(8,128)(2,1)S(1)} all-to-all(bf16[4,2,16,512]{3,2,1,0:T(8,128)(2,1)S(1)} %broadcast_in_dim.6), channel_id=1, replica_groups=mesh['zh'=2,'yh'=4,'yl'=2,'x'=4,'zl'=4,'c'=2] {'zl'}, dimensions={0} | all-to-all | bytes 262144 | tf_op jit(solution)/shard_map/all_to_all | solution.py:242
  13.9 0.9 %broadcast_in_dim.7 = bf16[4,4,2,16,512]{4,3,2,1,0:T(8,128)(2,1)} broadcast(bf16[4,2,16,512]{3,2,1,0:T(8,128)(2,1)S(1)} %all_to_all.20), dimensions={1,2,3,4} | broadcast | bytes 655360 | tf_op jit(solution)/shard_map/broadcast_in_dim | solution.py:242
  14.8 0.0 copy-start
  14.8 4.4 %all-to-all-start.1 = ((bf16[4,4,2,16,512]{4,3,2,1,0:T(8,128)(2,1)}), bf16[4,4,2,16,512]{4,3,2,1,0:T(8,128)(2,1)S(1)}, u32[]{:S(2)}, u32[]{:S(2)}) async-start(bf16[4,4,2,16,512]{4,3,2,1,0:T(8,128)(2,1)} %broadcast_in_dim.7), calls=%async_computation.1 | async-start | bytes 1048576 | tf_op jit(solution)/shard_map/all_to_all | solution.py:242
  19.2 0.0 copy-start.1
  19.2 8.1 %all-to-all-done.1 = bf16[4,4,2,16,512]{4,3,2,1,0:T(8,128)(2,1)S(1)} async-done(((bf16[4,4,2,16,512]{4,3,2,1,0:T(8,128)(2,1)}), bf16[4,4,2,16,512]{4,3,2,1,0:T(8,128)(2,1)S(1)}, u32[]{:S(2)}, u32[]{:S(2)}) %all-to-all-start.1) | async-done | bytes 524320 | tf_op jit(solution)/shard_map/all_to_all | solution.py:242
  27.3 0.0 copy-done
  27.3 0.0 copy-done.1
  27.3 27.8 %all_to_all.21 = f16[16,8,640]{2,1,0:T(8,128)(2,1)S(1)} all-to-all(f16[16,8,640]{2,1,0:T(8,128)(2,1)S(1)} %convert_bitcast_fusion), channel_id=1, replica_groups=mesh['zh'=2,'yh'=4,'yl'=2,'x'=4,'zl'=4,'c'=2] {'zh','yh','yl'}, dimensions={0} | all-to-all | bytes 327680 | tf_op jit(solution)/shard_map/all_to_all | solution.py:280
  55.1 0.1 slice_bitcast_fusion.2
  55.2 0.1 concatenate.3
  55.3 0.7 broadcast_in_dim.8
  56.0 5.0 %all-to-all-start.3 = ((f16[16,8,1152]{2,1,0:T(8,128)(2,1)}), f16[16,8,1152]{2,1,0:T(8,128)(2,1)S(1)}, u32[]{:S(2)}, u32[]{:S(2)}) async-start(f16[16,8,1152]{2,1,0:T(8,128)(2,1)} %broadcast_in_dim.8), calls=%async_computation.3 | async-start | bytes 589824 | tf_op jit(solution)/shard_map/all_to_all | solution.py:242
  61.1 1.9 %collective-permute-start.2 = (bf16[16,2,16,512]{3,2,1,0:T(8,128)(2,1)S(1)}, bf16[16,2,16,512]{3,2,1,0:T(8,128)(2,1)S(1)}, u32[]{:S(2)}, u32[]{:S(2)}) collective-permute-start(bf16[16,2,16,512]{3,2,1,0:T(8,128)(2,1)S(1)} %bitcast.15), channel_id=1, source_target_pairs={{64,65},{65,64},{96,97},{97,96},{128,129},{129,128},{160,161},{161... | collective-permute-start | bytes 1572872 | tf_op jit(solution)/shard_map/ppermute | solution.py:255
  63.0 11.5 %all-to-all-done.3 = f16[16,8,1152]{2,1,0:T(8,128)(2,1)S(1)} async-done(((f16[16,8,1152]{2,1,0:T(8,128)(2,1)}), f16[16,8,1152]{2,1,0:T(8,128)(2,1)S(1)}, u32[]{:S(2)}, u32[]{:S(2)}) %all-to-all-start.3) | async-done | bytes 294944 | tf_op jit(solution)/shard_map/all_to_all | solution.py:242
  74.6 0.0 collective-permute-done.2.other_ref
  74.6 1.4 %shard_map.41 = f32[512,128]{1,0:T(8,128)} custom-call(bf16[16,2,16,512]{3,2,1,0:T(8,128)(2,1)S(1)} %bitcast.16, bf16[16,2,16,512]{3,2,1,0:T(8,128)(2,1)S(1)} %collective-permute-done.2.other_ref, f32[16,8,1152]{2,1,0:T(8,128)S(1)} %convert_element_type.17.pieces_ref, f32[128,512]{1,0:T(8,128)S(1)} %get-tuple-element.24.x_ref, f32[512,128]{1,0:T(8,128)S(1)} %copy-done), custom_call_target="tpu_custom_call" | custom-call | tf_op jit(solution)/shard_map/pallas_call | solution.py:287
  (5 shorter events, 0.1 us)
Async XLA Ops:
  14.8 12.5 %copy-start = (f32[512,128]{1,0:T(8,128)S(1)}, f32[512,128]{1,0:T(8,128)}, u32[]{:S(2)}) copy-start(f32[512,128]{1,0:T(8,128)} %right_ref.1) | copy-start | bytes 786436
  14.8 12.5 %all-to-all-start.1 = ((bf16[4,4,2,16,512]{4,3,2,1,0:T(8,128)(2,1)}), bf16[4,4,2,16,512]{4,3,2,1,0:T(8,128)(2,1)S(1)}, u32[]{:S(2)}, u32[]{:S(2)}) async-start(bf16[4,4,2,16,512]{4,3,2,1,0:T(8,128)(2,1)} %broadcast_in_dim.7), calls=%async_computation.1 | async-start | bytes 1048576 | tf_op jit(solution)/shard_map/all_to_all | solution.py:242
  19.2 8.1 %copy-start.1 = (f32[2,512]{1,0:T(2,128)S(1)}, f32[2,512]{1,0:T(2,128)}, u32[]{:S(2)}) copy-start(f32[2,512]{1,0:T(2,128)} %param.6) | copy-start | bytes 12292
  56.0 18.5 %all-to-all-start.3 = ((f16[16,8,1152]{2,1,0:T(8,128)(2,1)}), f16[16,8,1152]{2,1,0:T(8,128)(2,1)S(1)}, u32[]{:S(2)}, u32[]{:S(2)}) async-start(f16[16,8,1152]{2,1,0:T(8,128)(2,1)} %broadcast_in_dim.8), calls=%async_computation.3 | async-start | bytes 589824 | tf_op jit(solution)/shard_map/all_to_all | solution.py:242
  61.1 13.5 %collective-permute-start.2 = (bf16[16,2,16,512]{3,2,1,0:T(8,128)(2,1)S(1)}, bf16[16,2,16,512]{3,2,1,0:T(8,128)(2,1)S(1)}, u32[]{:S(2)}, u32[]{:S(2)}) collective-permute-start(bf16[16,2,16,512]{3,2,1,0:T(8,128)(2,1)S(1)} %bitcast.15), channel_id=1, source_target_pairs={{64,65},{65,64},{96,97},{97,96},{128,129},{129,128},{160,161},{161... | collective-permute-start | bytes 1572872 | tf_op jit(solution)/shard_map/ppermute | solution.py:255

commit v8 on v7

--- a/solution.py
+++ b/solution.py
@@ -200,29 +200,38 @@
         out_sent_ref[...] = scaled(x)
 
 
-def last_kernel(own_ref, other_ref, pieces_ref, x_ref, right_ref, out_ref, panel_ref):
-    count, width, _ = panel_ref.shape
+def last_kernel(own_ref, other_ref, pieces_ref, x_ref, right_ref, out_ref, panel_ref, done_ref, sems):
+    count, width, rows = panel_ref.shape
     columns = x_ref.shape[0]
     me = lax.axis_index(ROW)
+    halves = [slice(i * BIG, (i + 1) * BIG) for i in range(rows // BIG)]
+    copies = [pltpu.make_async_copy(done_ref.at[h], out_ref.at[h], sems.at[i]) for i, h in enumerate(halves)]
 
     @pl.when(me < count)
     def _():
-        out_ref[...] = x_ref[...].T
+        for h, copy in zip(halves, copies):
+            done_ref[h] = x_ref[:, h].T
+            copy.start()
 
     @pl.when(me >= count)
     def _():
         assemble(panel_ref, own_ref, other_ref)
         got = pieces_ref[...].reshape(columns, count * width + BLK)
-        update = 0.0
+        parts = []
         for k in range(count):
-            parts = []
+            scaled_back = []
             for j in range(width // BLK):
                 at = k * width + j * BLK
                 lane = count * width + at * BLK // (count * width)
-                power = got[:, lane : lane + 1]
-                parts.append(got[:, at : at + BLK] * jnp.exp2(power - SPAN))
-            update = update + dot_exact_right(jnp.concatenate(parts, axis=1), panel_ref[k])
-        out_ref[...] = right_ref[...] - update.T
+                scaled_back.append(got[:, at : at + BLK] * jnp.exp2(got[:, lane : lane + 1] - SPAN))
+            parts.append(jnp.concatenate(split2(jnp.concatenate(scaled_back, axis=1)), axis=0))
+        for h, copy in zip(halves, copies):
+            both = sum(mm(parts[k], panel_ref[k, :, h]) for k in range(count))
+            done_ref[h] = right_ref[h] - (both[:columns] + both[columns:]).T
+            copy.start()
+
+    for copy in copies:
+        copy.wait()
 
 
 def on_chip(kernel, out_shape, n_in, scratch=()):
@@ -284,7 +293,15 @@
     pieces = same_to_all(mine, ROW).astype(F32)
     scratch = [pltpu.VMEM((count, width, rows), BF16)]
     out = jax.ShapeDtypeStruct((rows, columns), F32)
-    return on_chip(last_kernel, out, 5, scratch)(own, other_late, pieces, x, right)
+    vmem = pl.BlockSpec(memory_space=pltpu.VMEM)
+    return pl.pallas_call(
+        last_kernel,
+        out_shape=out,
+        in_specs=[vmem] * 5,
+        out_specs=pl.BlockSpec(memory_space=pl.ANY),
+        scratch_shapes=[*scratch, pltpu.VMEM((rows, columns), F32), pltpu.SemaphoreType.DMA((rows // BIG,))],
+        compiler_params=pltpu.CompilerParams(vmem_limit_bytes=24 * 1024 * 1024),
+    )(own, other_late, pieces, x, right)
 
 
 def solution(mesh):

time: 76.4 us -> 76.4 us (level)
  no operation moved by 1% of the time
where the time goes in v8:
time: 76.4 us; the launch traced here: 76 us
  blocking collectives  41 us (54%)
  waiting for transfers between devices  19.6 us (26%)
  starting transfers between devices  11.4 us (15%)
  local copies, waits for them, and re-layouts  2.54 us (3%)
  Pallas kernels  1.39 us (2%)
    all_to_all x1, blocking collectives, whole(): mine = lax.all_to_all(sent, ROW, 0, 0, tiled=True)[:count]  27.8 us
    all_to_all x2, waiting for transfers between devices, same_to_all(): lax.all_to_all(jnp.broadcast_to(piece[None], (count, *piece.shape)), axes...  19.6 us
    all_to_all x1, blocking collectives, same_to_all(): lax.all_to_all(jnp.broadcast_to(piece[None], (count, *piece.shape)), axes...  13.1 us
    all_to_all x2, starting transfers between devices, same_to_all(): lax.all_to_all(jnp.broadcast_to(piece[None], (count, *piece.shape)), axes...  9.45 us
    broadcast_in_dim x3, local copies, waits for them, and re-layouts, same_to_all(): jnp.broadcast_to(piece[None], (count, *piece.shape))  2.36 us
    ppermute x1, starting transfers between devices, whole(): other_late = lax.ppermute(own, ROW + ('c',), swap)  1.91 us
  transfers between devices with their start and end apart: 3, of which 2 were waited for; matrix products, arithmetic and copies ran while one was open for 0% of the time, Pallas kernels for 0%

profile of v8, /device:TPU:16, one launch (start us, length us, event | category | flops | bytes accessed | tf_op | source)
XLA Modules:
  0.0 76.0 jit_solution(14439454367076165040)
XLA Ops:
  0.0 0.8 %broadcast_in_dim.6 = bf16[4,2,16,512]{3,2,1,0:T(8,128)(2,1)S(1)} broadcast(bf16[2,16,512]{2,1,0:T(8,128)(2,1)} %bitcast.17), dimensions={1,2,3} | broadcast | bytes 163840 | tf_op jit(solution)/shard_map/broadcast_in_dim | solution.py:251
  0.8 13.1 %all_to_all.20 = bf16[4,2,16,512]{3,2,1,0:T(8,128)(2,1)S(1)} all-to-all(bf16[4,2,16,512]{3,2,1,0:T(8,128)(2,1)S(1)} %broadcast_in_dim.6), channel_id=1, replica_groups=mesh['zh'=2,'yh'=4,'yl'=2,'x'=4,'zl'=4,'c'=2] {'zl'}, dimensions={0} | all-to-all | bytes 262144 | tf_op jit(solution)/shard_map/all_to_all | solution.py:251
  13.9 0.9 %broadcast_in_dim.7 = bf16[4,4,2,16,512]{4,3,2,1,0:T(8,128)(2,1)} broadcast(bf16[4,2,16,512]{3,2,1,0:T(8,128)(2,1)S(1)} %all_to_all.20), dimensions={1,2,3,4} | broadcast | bytes 655360 | tf_op jit(solution)/shard_map/broadcast_in_dim | solution.py:251
  14.8 0.0 copy-start
  14.8 4.4 %all-to-all-start.1 = ((bf16[4,4,2,16,512]{4,3,2,1,0:T(8,128)(2,1)}), bf16[4,4,2,16,512]{4,3,2,1,0:T(8,128)(2,1)S(1)}, u32[]{:S(2)}, u32[]{:S(2)}) async-start(bf16[4,4,2,16,512]{4,3,2,1,0:T(8,128)(2,1)} %broadcast_in_dim.7), calls=%async_computation.1 | async-start | bytes 1048576 | tf_op jit(solution)/shard_map/all_to_all | solution.py:251
  19.2 0.0 copy-start.1
  19.2 8.1 %all-to-all-done.1 = bf16[4,4,2,16,512]{4,3,2,1,0:T(8,128)(2,1)S(1)} async-done(((bf16[4,4,2,16,512]{4,3,2,1,0:T(8,128)(2,1)}), bf16[4,4,2,16,512]{4,3,2,1,0:T(8,128)(2,1)S(1)}, u32[]{:S(2)}, u32[]{:S(2)}) %all-to-all-start.1) | async-done | bytes 524320 | tf_op jit(solution)/shard_map/all_to_all | solution.py:251
  27.3 0.0 copy-done
  27.3 0.0 copy-done.1
  27.3 27.8 %all_to_all.21 = f16[16,8,640]{2,1,0:T(8,128)(2,1)S(1)} all-to-all(f16[16,8,640]{2,1,0:T(8,128)(2,1)S(1)} %convert_bitcast_fusion), channel_id=1, replica_groups=mesh['zh'=2,'yh'=4,'yl'=2,'x'=4,'zl'=4,'c'=2] {'zh','yh','yl'}, dimensions={0} | all-to-all | bytes 327680 | tf_op jit(solution)/shard_map/all_to_all | solution.py:289
  55.1 0.1 slice_bitcast_fusion.2
  55.2 0.1 concatenate.3
  55.3 0.7 broadcast_in_dim.8
  56.0 5.0 %all-to-all-start.3 = ((f16[16,8,1152]{2,1,0:T(8,128)(2,1)}), f16[16,8,1152]{2,1,0:T(8,128)(2,1)S(1)}, u32[]{:S(2)}, u32[]{:S(2)}) async-start(f16[16,8,1152]{2,1,0:T(8,128)(2,1)} %broadcast_in_dim.8), calls=%async_computation.3 | async-start | bytes 589824 | tf_op jit(solution)/shard_map/all_to_all | solution.py:251
  61.1 1.9 %collective-permute-start.2 = (bf16[16,2,16,512]{3,2,1,0:T(8,128)(2,1)S(1)}, bf16[16,2,16,512]{3,2,1,0:T(8,128)(2,1)S(1)}, u32[]{:S(2)}, u32[]{:S(2)}) collective-permute-start(bf16[16,2,16,512]{3,2,1,0:T(8,128)(2,1)S(1)} %bitcast.15), channel_id=1, source_target_pairs={{64,65},{65,64},{96,97},{97,96},{128,129},{129,128},{160,161},{161... | collective-permute-start | bytes 1572872 | tf_op jit(solution)/shard_map/ppermute | solution.py:264
  63.0 11.5 %all-to-all-done.3 = f16[16,8,1152]{2,1,0:T(8,128)(2,1)S(1)} async-done(((f16[16,8,1152]{2,1,0:T(8,128)(2,1)}), f16[16,8,1152]{2,1,0:T(8,128)(2,1)S(1)}, u32[]{:S(2)}, u32[]{:S(2)}) %all-to-all-start.3) | async-done | bytes 294944 | tf_op jit(solution)/shard_map/all_to_all | solution.py:251
  74.6 0.0 collective-permute-done.2.other_ref
  74.6 1.4 %shard_map.41 = f32[512,128]{1,0:T(8,128)} custom-call(bf16[16,2,16,512]{3,2,1,0:T(8,128)(2,1)S(1)} %bitcast.16, bf16[16,2,16,512]{3,2,1,0:T(8,128)(2,1)S(1)} %collective-permute-done.2.other_ref, f32[16,8,1152]{2,1,0:T(8,128)S(1)} %convert_element_type.17.pieces_ref, f32[128,512]{1,0:T(8,128)S(1)} %get-tuple-element.24.x_ref, f32[512,128]{1,0:T(8,128)S(1)} %copy-done), custom_call_target="tpu_custom_call" | custom-call | tf_op jit(solution)/shard_map/pallas_call | solution.py:297
  (5 shorter events, 0.1 us)
Async XLA Ops:
  14.8 12.5 %copy-start = (f32[512,128]{1,0:T(8,128)S(1)}, f32[512,128]{1,0:T(8,128)}, u32[]{:S(2)}) copy-start(f32[512,128]{1,0:T(8,128)} %right_ref.1) | copy-start | bytes 786436
  14.8 12.5 %all-to-all-start.1 = ((bf16[4,4,2,16,512]{4,3,2,1,0:T(8,128)(2,1)}), bf16[4,4,2,16,512]{4,3,2,1,0:T(8,128)(2,1)S(1)}, u32[]{:S(2)}, u32[]{:S(2)}) async-start(bf16[4,4,2,16,512]{4,3,2,1,0:T(8,128)(2,1)} %broadcast_in_dim.7), calls=%async_computation.1 | async-start | bytes 1048576 | tf_op jit(solution)/shard_map/all_to_all | solution.py:251
  19.2 8.1 %copy-start.1 = (f32[2,512]{1,0:T(2,128)S(1)}, f32[2,512]{1,0:T(2,128)}, u32[]{:S(2)}) copy-start(f32[2,512]{1,0:T(2,128)} %param.6) | copy-start | bytes 12292
  56.0 18.5 %all-to-all-start.3 = ((f16[16,8,1152]{2,1,0:T(8,128)(2,1)}), f16[16,8,1152]{2,1,0:T(8,128)(2,1)S(1)}, u32[]{:S(2)}, u32[]{:S(2)}) async-start(f16[16,8,1152]{2,1,0:T(8,128)(2,1)} %broadcast_in_dim.8), calls=%async_computation.3 | async-start | bytes 589824 | tf_op jit(solution)/shard_map/all_to_all | solution.py:251
  61.1 13.5 %collective-permute-start.2 = (bf16[16,2,16,512]{3,2,1,0:T(8,128)(2,1)S(1)}, bf16[16,2,16,512]{3,2,1,0:T(8,128)(2,1)S(1)}, u32[]{:S(2)}, u32[]{:S(2)}) collective-permute-start(bf16[16,2,16,512]{3,2,1,0:T(8,128)(2,1)S(1)} %bitcast.15), channel_id=1, source_target_pairs={{64,65},{65,64},{96,97},{97,96},{128,129},{129,128},{160,161},{161... | collective-permute-start | bytes 1572872 | tf_op jit(solution)/shard_map/ppermute | solution.py:264

commit v9 on v7

--- a/solution.py
+++ b/solution.py
@@ -155,7 +155,7 @@
             into[pl.ds(pl.multiple_of((2 * g + 1 - core) * w, w), w)] = other_ref[g, k]
 
 
-def first_kernel(cols_ref, pivot_ref, right_ref, x_ref, sent_ref, hop_ref, panel_ref):
+def first_kernel(cols_ref, pivot_ref, right_ref, x_ref, hop_ref, panel_ref):
     cores, groups, w, _ = cols_ref.shape
     for g in range(groups):
         for c in range(cores):
@@ -167,7 +167,6 @@
         inverse = invert_panel(panel_ref, pivot_ref[0:1])
         x = substitute(inverse, lambda n, j: panel_ref[:n, j * BIG : (j + 1) * BIG], right_ref[...].T)
         x_ref[...] = x
-        sent_ref[...] = scaled(x)
         hop_ref[...] = scaled_rows(x)
 
 
@@ -180,14 +179,14 @@
 
 
 def second_kernel(
-    got_ref, own_ref, other_ref, panel_ref, inv_ref, turned_ref, x_ref, sent_ref, out_ref, out_sent_ref, low_ref
+    got_ref, own_ref, other_ref, panel_ref, inv_ref, turned_ref, x_ref, out_ref, out_sent_ref, low_ref
 ):
     me = lax.axis_index(ROW)
 
     @pl.when(me == 0)
     def _():
         out_ref[...] = x_ref[...]
-        out_sent_ref[...] = sent_ref[...]
+        out_sent_ref[...] = scaled(x_ref[...])
 
     @pl.when(me == 1)
     def _():
@@ -262,14 +261,14 @@
         both = lax.all_gather(mine, "c")
         other = jax.ShapeDtypeStruct((columns + 8, width), F32), jax.ShapeDtypeStruct((width, rows), BF16)
         kept = (jax.ShapeDtypeStruct((width // BIG, BIG, BIG), F32), jax.ShapeDtypeStruct((columns, width), F32))
-        x, sent, hop, panel = on_chip(first_kernel, solved + other, 3)(both, pivots, right)
+        x, hop, panel = on_chip(first_kernel, solved[:1] + other, 3)(both, pivots, right)
         got = lax.ppermute(hop.astype(jnp.float16), ROW, [(0, 1)])
         swap = [(2 * r + c, 2 * r + 1 - c) for r in range(count) for c in (0, 1)]
         low = lax.ppermute(rest, ROW + ("c",), swap)
         inverse, turned = on_chip(invert_kernel, kept, 3)(panel, pivots, right)
         scratch = [pltpu.VMEM((1, width, rows), BF16)]
-        return on_chip(second_kernel, solved, 8, scratch)(
-            got.astype(F32), rest, low, panel, inverse, turned, x, sent
+        return on_chip(second_kernel, solved, 7, scratch)(
+            got.astype(F32), rest, low, panel, inverse, turned, x
         )
 
     def skip(own, pivots, right):

time: 76.4 us -> 76.3 us (level)
  the two profiles are of different devices: /device:TPU:16 before, /device:TPU:8 now
where the time goes in v9:
time: 76.3 us; the launch traced here: 75.9 us
  blocking collectives  30.9 us (40%)
  waiting for transfers between devices  26.5 us (35%)
  starting transfers between devices  12.3 us (16%)
  Pallas kernels  3.4 us (4%)
  local copies, waits for them, and re-layouts  2.58 us (3%)
    all_to_all x2, waiting for transfers between devices, same_to_all(): lax.all_to_all(jnp.broadcast_to(piece[None], (count, *piece.shape)), axes...  21.3 us
    all_to_all x1, blocking collectives, whole(): mine = lax.all_to_all(sent, ROW, 0, 0, tiled=True)[:count]  15.5 us
    all_to_all x1, blocking collectives, same_to_all(): lax.all_to_all(jnp.broadcast_to(piece[None], (count, *piece.shape)), axes...  13.1 us
    all_to_all x2, starting transfers between devices, same_to_all(): lax.all_to_all(jnp.broadcast_to(piece[None], (count, *piece.shape)), axes...  8.4 us
    ppermute x1, waiting for transfers between devices, solve(): got = lax.ppermute(hop.astype(jnp.float16), ROW, [(0, 1)])  5.21 us
    broadcast_in_dim x3, local copies, waits for them, and re-layouts, same_to_all(): jnp.broadcast_to(piece[None], (count, *piece.shape))  2.36 us
    all_gather x1, blocking collectives, solve(): both = lax.all_gather(mine, 'c')  2.31 us
    ppermute x1, starting transfers between devices, solve(): low = lax.ppermute(rest, ROW + ('c',), swap)  1.92 us
  transfers between devices with their start and end apart: 5, of which 3 were waited for; matrix products, arithmetic and copies ran while one was open for 0% of the time, Pallas kernels for 2%

profile of v9, /device:TPU:8, one launch (start us, length us, event | category | flops | bytes accessed | tf_op | source)
XLA Modules:
  0.0 75.9 jit_solution(5457410945405192024)
XLA Ops:
  0.0 0.8 %broadcast_in_dim.6 = bf16[4,2,16,512]{3,2,1,0:T(8,128)(2,1)S(1)} broadcast(bf16[2,16,512]{2,1,0:T(8,128)(2,1)} %bitcast.17), dimensions={1,2,3} | broadcast | bytes 163840 | tf_op jit(solution)/shard_map/broadcast_in_dim | solution.py:241
  0.8 13.1 %all_to_all.20 = bf16[4,2,16,512]{3,2,1,0:T(8,128)(2,1)S(1)} all-to-all(bf16[4,2,16,512]{3,2,1,0:T(8,128)(2,1)S(1)} %broadcast_in_dim.6), channel_id=1, replica_groups=mesh['zh'=2,'yh'=4,'yl'=2,'x'=4,'zl'=4,'c'=2] {'zl'}, dimensions={0} | all-to-all | bytes 262144 | tf_op jit(solution)/shard_map/all_to_all | solution.py:241
  13.9 0.9 %broadcast_in_dim.7 = bf16[4,4,2,16,512]{4,3,2,1,0:T(8,128)(2,1)} broadcast(bf16[4,2,16,512]{3,2,1,0:T(8,128)(2,1)S(1)} %all_to_all.20), dimensions={1,2,3,4} | broadcast | bytes 655360 | tf_op jit(solution)/shard_map/broadcast_in_dim | solution.py:241
  14.8 0.0 copy-start
  14.8 4.4 %all-to-all-start.1 = ((bf16[4,4,2,16,512]{4,3,2,1,0:T(8,128)(2,1)}), bf16[4,4,2,16,512]{4,3,2,1,0:T(8,128)(2,1)S(1)}, u32[]{:S(2)}, u32[]{:S(2)}) async-start(bf16[4,4,2,16,512]{4,3,2,1,0:T(8,128)(2,1)} %broadcast_in_dim.7), calls=%async_computation.1 | async-start | bytes 1048576 | tf_op jit(solution)/shard_map/all_to_all | solution.py:241
  19.2 0.0 copy-start.1
  19.2 8.1 %all-to-all-done.1 = bf16[4,4,2,16,512]{4,3,2,1,0:T(8,128)(2,1)S(1)} async-done(((bf16[4,4,2,16,512]{4,3,2,1,0:T(8,128)(2,1)}), bf16[4,4,2,16,512]{4,3,2,1,0:T(8,128)(2,1)S(1)}, u32[]{:S(2)}, u32[]{:S(2)}) %all-to-all-start.1) | async-done | bytes 524320 | tf_op jit(solution)/shard_map/all_to_all | solution.py:241
  27.3 0.0 copy-done
  27.3 0.0 copy-done.1
  27.3 13.4 %conditional.1 = ((f32[128,512]{1,0:T(8,128)S(1)}, f32[128,640]{1,0:T(8,128)S(1)})) conditional(s32[]{:T(128)} %convert_element_type.15, f32[512,128]{1,0:T(8,128)S(1)} %copy-done, (bf16[16,2,16,512]{3,2,1,0:T(8,128)(2,1)S(1)}, f32[2,512]{1,0:T(2,128)S(1)}, f32[512,128]{1,0:T(8,128)S(1)}) %tuple.21), branch_computations={%region_0.0_spmd, %region_1.2_spmd} | conditional | flops 139284 | bytes 4276544 | solution.py:277
  27.3 1.9 %collective-permute-start.1 = (bf16[16,1,16,512]{3,2,1,0:T(8,128)(2,1)S(1)}, bf16[16,1,16,512]{3,2,1,0:T(8,128)(2,1)S(1)}, u32[]{:S(2)}, u32[]{:S(2)}) collective-permute-start(bf16[16,1,16,512]{3,2,1,0:T(8,128)(2,1)S(1)} %get-tuple-element.26.own_ref), channel_id=1, source_target_pairs={{0,1},{1,0},{32,33},{33,32},{2,3},{3,2},{34,35},{35,34},{4,5},{5,4... | collective-permute-start | bytes 786440 | tf_op jit(solution)/shard_map/cond/branch_1_fun/ppermute | solution.py:267
  29.2 2.3 %all-gather = bf16[32,1,16,512]{3,2,1,0:T(8,128)(2,1)S(1)} all-gather(bf16[16,1,16,512]{3,2,1,0:T(8,128)(2,1)S(1)} %get-tuple-element.27), channel_id=2, replica_groups=mesh['zh'=2,'yh'=4,'yl'=2,'x'=4,'zl'=4,'c'=2] {'c'}, dimensions={0}, use_global_device_ids=true | all-gather | bytes 786432 | tf_op jit(solution)/shard_map/cond/branch_1_fun/all_gather | solution.py:261
  31.6 1.3 %collective-permute-start = (f16[136,512]{1,0:T(8,128)(2,1)S(1)}, f16[136,512]{1,0:T(8,128)(2,1)S(1)}, u32[]{:S(2)}, u32[]{:S(2)}) collective-permute-start(f16[136,512]{1,0:T(8,128)(2,1)S(1)} %convert_element_type.10), channel_id=1, source_target_pairs={{0,32},{1,33},{2,34},{3,35},{4,36},{5,37},{6,38},{7,39},{8,40},{9,... | collective-permute-start | bytes 417800 | tf_op jit(solution)/shard_map/cond/branch_1_fun/ppermute | solution.py:265
  32.9 1.5 %branch_1_fun.4 = (f32[2,256,256]{2,1,0:T(8,128)S(1)}, f32[128,512]{1,0:T(8,128)S(1)}) custom-call(bf16[512,512]{1,0:T(8,128)(2,1)S(1)} %get-tuple-element.16.panel_ref, f32[2,512]{1,0:T(2,128)S(1)} %get-tuple-element.25.pivot_ref, f32[512,128]{1,0:T(8,128)S(1)} %get-tuple-element.14.right_ref), custom_call_target="tpu_custom_call" | custom-call | tf_op jit(solution)/shard_map/cond/branch_1_fun/pallas_call | solution.py:268
  34.5 5.2 %collective-permute-done = f16[136,512]{1,0:T(8,128)(2,1)S(1)} collective-permute-done((f16[136,512]{1,0:T(8,128)(2,1)S(1)}, f16[136,512]{1,0:T(8,128)(2,1)S(1)}, u32[]{:S(2)}, u32[]{:S(2)}) %collective-permute-start) | collective-permute-done | bytes 139296 | tf_op jit(solution)/shard_map/cond/branch_1_fun/ppermute | solution.py:265
  39.7 0.0 collective-permute-done.1.other_ref
  39.7 1.0 %branch_1_fun.5 = (f32[128,512]{1,0:T(8,128)S(1)}, f32[128,640]{1,0:T(8,128)S(1)}) custom-call(f32[136,512]{1,0:T(8,128)S(1)} %convert_element_type.11.got_ref, bf16[16,1,16,512]{3,2,1,0:T(8,128)(2,1)S(1)} %get-tuple-element.26.own_ref, bf16[16,1,16,512]{3,2,1,0:T(8,128)(2,1)S(1)} %collective-permute-done.1.other_ref, ...), custom_call_target="tpu_custom_call" | custom-call | tf_op jit(solution)/shard_map/cond/branch_1_fun/pallas_call | solution.py:270
  40.7 15.5 %all_to_all.21 = f16[16,8,640]{2,1,0:T(8,128)(2,1)S(1)} all-to-all(f16[16,8,640]{2,1,0:T(8,128)(2,1)S(1)} %convert_bitcast_fusion), channel_id=1, replica_groups=mesh['zh'=2,'yh'=4,'yl'=2,'x'=4,'zl'=4,'c'=2] {'zh','yh','yl'}, dimensions={0} | all-to-all | bytes 327680 | tf_op jit(solution)/shard_map/all_to_all | solution.py:279
  56.2 0.1 slice_bitcast_fusion.2
  56.3 0.1 concatenate.3
  56.4 0.7 broadcast_in_dim.8
  57.1 4.0 %all-to-all-start.3 = ((f16[16,8,1152]{2,1,0:T(8,128)(2,1)}), f16[16,8,1152]{2,1,0:T(8,128)(2,1)S(1)}, u32[]{:S(2)}, u32[]{:S(2)}) async-start(f16[16,8,1152]{2,1,0:T(8,128)(2,1)} %broadcast_in_dim.8), calls=%async_computation.3 | async-start | bytes 589824 | tf_op jit(solution)/shard_map/all_to_all | solution.py:241
  61.1 0.7 collective-permute-start.2
  61.8 13.2 %all-to-all-done.3 = f16[16,8,1152]{2,1,0:T(8,128)(2,1)S(1)} async-done(((f16[16,8,1152]{2,1,0:T(8,128)(2,1)}), f16[16,8,1152]{2,1,0:T(8,128)(2,1)S(1)}, u32[]{:S(2)}, u32[]{:S(2)}) %all-to-all-start.3) | async-done | bytes 294944 | tf_op jit(solution)/shard_map/all_to_all | solution.py:241
  75.0 0.0 collective-permute-done.2.other_ref
  75.0 0.9 %shard_map.41 = f32[512,128]{1,0:T(8,128)} custom-call(bf16[16,2,16,512]{3,2,1,0:T(8,128)(2,1)S(1)} %bitcast.16, bf16[16,2,16,512]{3,2,1,0:T(8,128)(2,1)S(1)} %collective-permute-done.2.other_ref, f32[16,8,1152]{2,1,0:T(8,128)S(1)} %convert_element_type.17.pieces_ref, f32[128,512]{1,0:T(8,128)S(1)} %get-tuple-element.23.x_ref, f32[512,128]{1,0:T(8,128)S(1)} %copy-done), custom_call_target="tpu_custom_call" | custom-call | tf_op jit(solution)/shard_map/pallas_call | solution.py:286
  (7 shorter events, 0.2 us)
Async XLA Ops:
  14.8 12.5 %copy-start = (f32[512,128]{1,0:T(8,128)S(1)}, f32[512,128]{1,0:T(8,128)}, u32[]{:S(2)}) copy-start(f32[512,128]{1,0:T(8,128)} %right_ref.1) | copy-start | bytes 786436
  14.8 12.5 %all-to-all-start.1 = ((bf16[4,4,2,16,512]{4,3,2,1,0:T(8,128)(2,1)}), bf16[4,4,2,16,512]{4,3,2,1,0:T(8,128)(2,1)S(1)}, u32[]{:S(2)}, u32[]{:S(2)}) async-start(bf16[4,4,2,16,512]{4,3,2,1,0:T(8,128)(2,1)} %broadcast_in_dim.7), calls=%async_computation.1 | async-start | bytes 1048576 | tf_op jit(solution)/shard_map/all_to_all | solution.py:241
  19.2 8.1 %copy-start.1 = (f32[2,512]{1,0:T(2,128)S(1)}, f32[2,512]{1,0:T(2,128)}, u32[]{:S(2)}) copy-start(f32[2,512]{1,0:T(2,128)} %param.6) | copy-start | bytes 12292
  27.3 12.4 %collective-permute-start.1 = (bf16[16,1,16,512]{3,2,1,0:T(8,128)(2,1)S(1)}, bf16[16,1,16,512]{3,2,1,0:T(8,128)(2,1)S(1)}, u32[]{:S(2)}, u32[]{:S(2)}) collective-permute-start(bf16[16,1,16,512]{3,2,1,0:T(8,128)(2,1)S(1)} %get-tuple-element.26.own_ref), channel_id=1, source_target_pairs={{0,1},{1,0},{32,33},{33,32},{2,3},{3,2},{34,35},{35,34},{4,5},{5,4... | collective-permute-start | bytes 786440 | tf_op jit(solution)/shard_map/cond/branch_1_fun/ppermute | solution.py:267
  31.6 8.0 %collective-permute-start = (f16[136,512]{1,0:T(8,128)(2,1)S(1)}, f16[136,512]{1,0:T(8,128)(2,1)S(1)}, u32[]{:S(2)}, u32[]{:S(2)}) collective-permute-start(f16[136,512]{1,0:T(8,128)(2,1)S(1)} %convert_element_type.10), channel_id=1, source_target_pairs={{0,32},{1,33},{2,34},{3,35},{4,36},{5,37},{6,38},{7,39},{8,40},{9,... | collective-permute-start | bytes 417800 | tf_op jit(solution)/shard_map/cond/branch_1_fun/ppermute | solution.py:265
  57.1 17.9 %all-to-all-start.3 = ((f16[16,8,1152]{2,1,0:T(8,128)(2,1)}), f16[16,8,1152]{2,1,0:T(8,128)(2,1)S(1)}, u32[]{:S(2)}, u32[]{:S(2)}) async-start(f16[16,8,1152]{2,1,0:T(8,128)(2,1)} %broadcast_in_dim.8), calls=%async_computation.3 | async-start | bytes 589824 | tf_op jit(solution)/shard_map/all_to_all | solution.py:241
  61.1 13.9 %collective-permute-start.2 = (bf16[16,2,16,512]{3,2,1,0:T(8,128)(2,1)S(1)}, bf16[16,2,16,512]{3,2,1,0:T(8,128)(2,1)S(1)}, u32[]{:S(2)}, u32[]{:S(2)}) collective-permute-start(bf16[16,2,16,512]{3,2,1,0:T(8,128)(2,1)S(1)} %bitcast.15), channel_id=1, source_target_pairs={{64,65},{65,64},{96,97},{97,96},{128,129},{129,128},{160,161},{161... | collective-permute-start | bytes 1572872 | tf_op jit(solution)/shard_map/ppermute | solution.py:254

commit v10 on v9

--- a/solution.py
+++ b/solution.py
@@ -24,12 +24,6 @@
     return lax.dot_general(a, b, (((1,), (1 if trans else 0,)), ((), ())), preferred_element_type=F32)
 
 
-def dot_exact_left(a, v):
-    n = v.shape[1]
-    both = mm(a, jnp.concatenate(split2(v), axis=1))
-    return both[:, :n] + both[:, n:]
-
-
 def dot_exact_right(v, b):
     m = v.shape[0]
     both = mm(jnp.concatenate(split2(v), axis=0), b)
@@ -42,6 +36,20 @@
     bh, bl = split2(b)
     both = mm(jnp.concatenate([ah, al], axis=0), bh, trans)
     return both[:m] + (both[m:] + mm(ah, bl, trans))
+
+
+def deep_left(a, v):
+    return mm(jnp.concatenate([a, a], axis=1), jnp.concatenate(split2(v), axis=0))
+
+
+def deep_right(v, b):
+    return mm(jnp.concatenate(split2(v), axis=1), jnp.concatenate([b, b], axis=0))
+
+
+def deep3(a, b):
+    ah, al = split2(a)
+    bh, bl = split2(b)
+    return mm(jnp.concatenate([ah, al, ah], axis=1), jnp.concatenate([bh, bh, bl], axis=0))
 
 
 def iota(shape, dim):
@@ -92,14 +100,14 @@
     size = BASE
     while size < BLK:
         off = (row // size > lane // size) & (row // (2 * size) == lane // (2 * size))
-        half = [dot_exact_right(x, jnp.where(off, blk, 0.0).astype(BF16)) for x, blk in zip(out, low)]
-        out = [x - dot3(h, x) for x, h in zip(out, half)]
+        half = [deep_right(x, jnp.where(off, blk, 0.0).astype(BF16)) for x, blk in zip(out, low)]
+        out = [x - deep3(h, x) for x, h in zip(out, half)]
         size *= 2
     return out
 
 
 def join_blocks(first, second, low):
-    off = -dot3(second, dot_exact_left(low, first))
+    off = -deep3(second, deep_left(low, first))
     top = jnp.concatenate([first, jnp.zeros_like(first)], axis=1)
     return jnp.concatenate([top, jnp.concatenate([off, second], axis=1)], axis=0)
 

time: 76.3 us -> 76.3 us (level)
  no operation moved by 1% of the time
where the time goes in v10:
time: 76.3 us; the launch traced here: 75.8 us
  blocking collectives  30.9 us (40%)
  waiting for transfers between devices  26.5 us (35%)
  starting transfers between devices  12.3 us (16%)
  Pallas kernels  3.44 us (5%)
  local copies, waits for them, and re-layouts  2.58 us (3%)
    all_to_all x2, waiting for transfers between devices, same_to_all(): lax.all_to_all(jnp.broadcast_to(piece[None], (count, *piece.shape)), axes...  21.3 us
    all_to_all x1, blocking collectives, whole(): mine = lax.all_to_all(sent, ROW, 0, 0, tiled=True)[:count]  15.4 us
    all_to_all x1, blocking collectives, same_to_all(): lax.all_to_all(jnp.broadcast_to(piece[None], (count, *piece.shape)), axes...  13.1 us
    all_to_all x2, starting transfers between devices, same_to_all(): lax.all_to_all(jnp.broadcast_to(piece[None], (count, *piece.shape)), axes...  8.4 us
    ppermute x1, waiting for transfers between devices, solve(): got = lax.ppermute(hop.astype(jnp.float16), ROW, [(0, 1)])  5.13 us
    broadcast_in_dim x3, local copies, waits for them, and re-layouts, same_to_all(): jnp.broadcast_to(piece[None], (count, *piece.shape))  2.36 us
    all_gather x1, blocking collectives, solve(): both = lax.all_gather(mine, 'c')  2.31 us
    ppermute x1, starting transfers between devices, solve(): low = lax.ppermute(rest, ROW + ('c',), swap)  1.92 us
  transfers between devices with their start and end apart: 5, of which 3 were waited for; matrix products, arithmetic and copies ran while one was open for 0% of the time, Pallas kernels for 2%

profile of v10, /device:TPU:8, one launch (start us, length us, event | category | flops | bytes accessed | tf_op | source)
XLA Modules:
  0.0 75.8 jit_solution(15401066698143283722)
XLA Ops:
  0.0 0.8 %broadcast_in_dim.6 = bf16[4,2,16,512]{3,2,1,0:T(8,128)(2,1)S(1)} broadcast(bf16[2,16,512]{2,1,0:T(8,128)(2,1)} %bitcast.17), dimensions={1,2,3} | broadcast | bytes 163840 | tf_op jit(solution)/shard_map/broadcast_in_dim | solution.py:249
  0.8 13.1 %all_to_all.20 = bf16[4,2,16,512]{3,2,1,0:T(8,128)(2,1)S(1)} all-to-all(bf16[4,2,16,512]{3,2,1,0:T(8,128)(2,1)S(1)} %broadcast_in_dim.6), channel_id=1, replica_groups=mesh['zh'=2,'yh'=4,'yl'=2,'x'=4,'zl'=4,'c'=2] {'zl'}, dimensions={0} | all-to-all | bytes 262144 | tf_op jit(solution)/shard_map/all_to_all | solution.py:249
  13.9 0.9 %broadcast_in_dim.7 = bf16[4,4,2,16,512]{4,3,2,1,0:T(8,128)(2,1)} broadcast(bf16[4,2,16,512]{3,2,1,0:T(8,128)(2,1)S(1)} %all_to_all.20), dimensions={1,2,3,4} | broadcast | bytes 655360 | tf_op jit(solution)/shard_map/broadcast_in_dim | solution.py:249
  14.8 0.0 copy-start
  14.8 4.4 %all-to-all-start.1 = ((bf16[4,4,2,16,512]{4,3,2,1,0:T(8,128)(2,1)}), bf16[4,4,2,16,512]{4,3,2,1,0:T(8,128)(2,1)S(1)}, u32[]{:S(2)}, u32[]{:S(2)}) async-start(bf16[4,4,2,16,512]{4,3,2,1,0:T(8,128)(2,1)} %broadcast_in_dim.7), calls=%async_computation.1 | async-start | bytes 1048576 | tf_op jit(solution)/shard_map/all_to_all | solution.py:249
  19.2 0.0 copy-start.1
  19.2 8.1 %all-to-all-done.1 = bf16[4,4,2,16,512]{4,3,2,1,0:T(8,128)(2,1)S(1)} async-done(((bf16[4,4,2,16,512]{4,3,2,1,0:T(8,128)(2,1)}), bf16[4,4,2,16,512]{4,3,2,1,0:T(8,128)(2,1)S(1)}, u32[]{:S(2)}, u32[]{:S(2)}) %all-to-all-start.1) | async-done | bytes 524320 | tf_op jit(solution)/shard_map/all_to_all | solution.py:249
  27.3 0.0 copy-done
  27.3 0.0 copy-done.1
  27.3 13.4 %conditional.1 = ((f32[128,512]{1,0:T(8,128)S(1)}, f32[128,640]{1,0:T(8,128)S(1)})) conditional(s32[]{:T(128)} %convert_element_type.15, f32[512,128]{1,0:T(8,128)S(1)} %copy-done, (bf16[16,2,16,512]{3,2,1,0:T(8,128)(2,1)S(1)}, f32[2,512]{1,0:T(2,128)S(1)}, f32[512,128]{1,0:T(8,128)S(1)}) %tuple.21), branch_computations={%region_0.0_spmd, %region_1.2_spmd} | conditional | flops 139284 | bytes 4276544 | solution.py:285
  27.3 1.9 %collective-permute-start.1 = (bf16[16,1,16,512]{3,2,1,0:T(8,128)(2,1)S(1)}, bf16[16,1,16,512]{3,2,1,0:T(8,128)(2,1)S(1)}, u32[]{:S(2)}, u32[]{:S(2)}) collective-permute-start(bf16[16,1,16,512]{3,2,1,0:T(8,128)(2,1)S(1)} %get-tuple-element.26.own_ref), channel_id=1, source_target_pairs={{0,1},{1,0},{32,33},{33,32},{2,3},{3,2},{34,35},{35,34},{4,5},{5,4... | collective-permute-start | bytes 786440 | tf_op jit(solution)/shard_map/cond/branch_1_fun/ppermute | solution.py:275
  29.2 2.3 %all-gather = bf16[32,1,16,512]{3,2,1,0:T(8,128)(2,1)S(1)} all-gather(bf16[16,1,16,512]{3,2,1,0:T(8,128)(2,1)S(1)} %get-tuple-element.27), channel_id=2, replica_groups=mesh['zh'=2,'yh'=4,'yl'=2,'x'=4,'zl'=4,'c'=2] {'c'}, dimensions={0}, use_global_device_ids=true | all-gather | bytes 786432 | tf_op jit(solution)/shard_map/cond/branch_1_fun/all_gather | solution.py:269
  31.6 1.3 %collective-permute-start = (f16[136,512]{1,0:T(8,128)(2,1)S(1)}, f16[136,512]{1,0:T(8,128)(2,1)S(1)}, u32[]{:S(2)}, u32[]{:S(2)}) collective-permute-start(f16[136,512]{1,0:T(8,128)(2,1)S(1)} %convert_element_type.10), channel_id=1, source_target_pairs={{0,32},{1,33},{2,34},{3,35},{4,36},{5,37},{6,38},{7,39},{8,40},{9,... | collective-permute-start | bytes 417800 | tf_op jit(solution)/shard_map/cond/branch_1_fun/ppermute | solution.py:273
  32.9 1.6 %branch_1_fun.4 = (f32[2,256,256]{2,1,0:T(8,128)S(1)}, f32[128,512]{1,0:T(8,128)S(1)}) custom-call(bf16[512,512]{1,0:T(8,128)(2,1)S(1)} %get-tuple-element.16.panel_ref, f32[2,512]{1,0:T(2,128)S(1)} %get-tuple-element.25.pivot_ref, f32[512,128]{1,0:T(8,128)S(1)} %get-tuple-element.14.right_ref), custom_call_target="tpu_custom_call" | custom-call | tf_op jit(solution)/shard_map/cond/branch_1_fun/pallas_call | solution.py:276
  34.5 5.1 %collective-permute-done = f16[136,512]{1,0:T(8,128)(2,1)S(1)} collective-permute-done((f16[136,512]{1,0:T(8,128)(2,1)S(1)}, f16[136,512]{1,0:T(8,128)(2,1)S(1)}, u32[]{:S(2)}, u32[]{:S(2)}) %collective-permute-start) | collective-permute-done | bytes 139296 | tf_op jit(solution)/shard_map/cond/branch_1_fun/ppermute | solution.py:273
  39.7 0.0 collective-permute-done.1.other_ref
  39.7 1.0 %branch_1_fun.5 = (f32[128,512]{1,0:T(8,128)S(1)}, f32[128,640]{1,0:T(8,128)S(1)}) custom-call(f32[136,512]{1,0:T(8,128)S(1)} %convert_element_type.11.got_ref, bf16[16,1,16,512]{3,2,1,0:T(8,128)(2,1)S(1)} %get-tuple-element.26.own_ref, bf16[16,1,16,512]{3,2,1,0:T(8,128)(2,1)S(1)} %collective-permute-done.1.other_ref, ...), custom_call_target="tpu_custom_call" | custom-call | tf_op jit(solution)/shard_map/cond/branch_1_fun/pallas_call | solution.py:278
  40.7 15.4 %all_to_all.21 = f16[16,8,640]{2,1,0:T(8,128)(2,1)S(1)} all-to-all(f16[16,8,640]{2,1,0:T(8,128)(2,1)S(1)} %convert_bitcast_fusion), channel_id=1, replica_groups=mesh['zh'=2,'yh'=4,'yl'=2,'x'=4,'zl'=4,'c'=2] {'zh','yh','yl'}, dimensions={0} | all-to-all | bytes 327680 | tf_op jit(solution)/shard_map/all_to_all | solution.py:287
  56.1 0.1 slice_bitcast_fusion.2
  56.2 0.1 concatenate.3
  56.3 0.7 broadcast_in_dim.8
  57.0 4.0 %all-to-all-start.3 = ((f16[16,8,1152]{2,1,0:T(8,128)(2,1)}), f16[16,8,1152]{2,1,0:T(8,128)(2,1)S(1)}, u32[]{:S(2)}, u32[]{:S(2)}) async-start(f16[16,8,1152]{2,1,0:T(8,128)(2,1)} %broadcast_in_dim.8), calls=%async_computation.3 | async-start | bytes 589824 | tf_op jit(solution)/shard_map/all_to_all | solution.py:249
  61.0 0.7 collective-permute-start.2
  61.7 13.3 %all-to-all-done.3 = f16[16,8,1152]{2,1,0:T(8,128)(2,1)S(1)} async-done(((f16[16,8,1152]{2,1,0:T(8,128)(2,1)}), f16[16,8,1152]{2,1,0:T(8,128)(2,1)S(1)}, u32[]{:S(2)}, u32[]{:S(2)}) %all-to-all-start.3) | async-done | bytes 294944 | tf_op jit(solution)/shard_map/all_to_all | solution.py:249
  75.0 0.0 collective-permute-done.2.other_ref
  75.0 0.9 %shard_map.41 = f32[512,128]{1,0:T(8,128)} custom-call(bf16[16,2,16,512]{3,2,1,0:T(8,128)(2,1)S(1)} %bitcast.16, bf16[16,2,16,512]{3,2,1,0:T(8,128)(2,1)S(1)} %collective-permute-done.2.other_ref, f32[16,8,1152]{2,1,0:T(8,128)S(1)} %convert_element_type.17.pieces_ref, f32[128,512]{1,0:T(8,128)S(1)} %get-tuple-element.23.x_ref, f32[512,128]{1,0:T(8,128)S(1)} %copy-done), custom_call_target="tpu_custom_call" | custom-call | tf_op jit(solution)/shard_map/pallas_call | solution.py:294
  (7 shorter events, 0.2 us)
Async XLA Ops:
  14.8 12.5 %copy-start = (f32[512,128]{1,0:T(8,128)S(1)}, f32[512,128]{1,0:T(8,128)}, u32[]{:S(2)}) copy-start(f32[512,128]{1,0:T(8,128)} %right_ref.1) | copy-start | bytes 786436
  14.8 12.5 %all-to-all-start.1 = ((bf16[4,4,2,16,512]{4,3,2,1,0:T(8,128)(2,1)}), bf16[4,4,2,16,512]{4,3,2,1,0:T(8,128)(2,1)S(1)}, u32[]{:S(2)}, u32[]{:S(2)}) async-start(bf16[4,4,2,16,512]{4,3,2,1,0:T(8,128)(2,1)} %broadcast_in_dim.7), calls=%async_computation.1 | async-start | bytes 1048576 | tf_op jit(solution)/shard_map/all_to_all | solution.py:249
  19.2 8.1 %copy-start.1 = (f32[2,512]{1,0:T(2,128)S(1)}, f32[2,512]{1,0:T(2,128)}, u32[]{:S(2)}) copy-start(f32[2,512]{1,0:T(2,128)} %param.6) | copy-start | bytes 12292
  27.3 12.3 %collective-permute-start.1 = (bf16[16,1,16,512]{3,2,1,0:T(8,128)(2,1)S(1)}, bf16[16,1,16,512]{3,2,1,0:T(8,128)(2,1)S(1)}, u32[]{:S(2)}, u32[]{:S(2)}) collective-permute-start(bf16[16,1,16,512]{3,2,1,0:T(8,128)(2,1)S(1)} %get-tuple-element.26.own_ref), channel_id=1, source_target_pairs={{0,1},{1,0},{32,33},{33,32},{2,3},{3,2},{34,35},{35,34},{4,5},{5,4... | collective-permute-start | bytes 786440 | tf_op jit(solution)/shard_map/cond/branch_1_fun/ppermute | solution.py:275
  31.6 8.0 %collective-permute-start = (f16[136,512]{1,0:T(8,128)(2,1)S(1)}, f16[136,512]{1,0:T(8,128)(2,1)S(1)}, u32[]{:S(2)}, u32[]{:S(2)}) collective-permute-start(f16[136,512]{1,0:T(8,128)(2,1)S(1)} %convert_element_type.10), channel_id=1, source_target_pairs={{0,32},{1,33},{2,34},{3,35},{4,36},{5,37},{6,38},{7,39},{8,40},{9,... | collective-permute-start | bytes 417800 | tf_op jit(solution)/shard_map/cond/branch_1_fun/ppermute | solution.py:273
  57.0 17.9 %all-to-all-start.3 = ((f16[16,8,1152]{2,1,0:T(8,128)(2,1)}), f16[16,8,1152]{2,1,0:T(8,128)(2,1)S(1)}, u32[]{:S(2)}, u32[]{:S(2)}) async-start(f16[16,8,1152]{2,1,0:T(8,128)(2,1)} %broadcast_in_dim.8), calls=%async_computation.3 | async-start | bytes 589824 | tf_op jit(solution)/shard_map/all_to_all | solution.py:249
  61.0 14.0 %collective-permute-start.2 = (bf16[16,2,16,512]{3,2,1,0:T(8,128)(2,1)S(1)}, bf16[16,2,16,512]{3,2,1,0:T(8,128)(2,1)S(1)}, u32[]{:S(2)}, u32[]{:S(2)}) collective-permute-start(bf16[16,2,16,512]{3,2,1,0:T(8,128)(2,1)S(1)} %bitcast.15), channel_id=1, source_target_pairs={{64,65},{65,64},{96,97},{97,96},{128,129},{129,128},{160,161},{161... | collective-permute-start | bytes 1572872 | tf_op jit(solution)/shard_map/ppermute | solution.py:262
